TPU v7x, 768 devices: a whole 4x8x12 slice. The times are simulated.
768 devices in a mesh: dp: 96 (over z, x, core), mp: 8 (over y).
Axes of the slice: x: 4, y: 8, z: 12, core: 2. Of those that a mesh axis runs over, the one named last changes fastest.
Arguments:
- partial_grads: bfloat16 [96, 1536, 4096], P('dp', None, 'mp'), may hold values from -1.25 to 1.25
- band_owner: int32 [96], replicated, may hold values from 0 to 95, as said below
- left_factor: float32 [1536, 4096], P('dp', 'mp'), may hold values from -1 to 2.5
- right_factor: float32 [1536, 4096], P('dp', 'mp'), may hold values from -1 to 2.5
- left_root: bfloat16 [1536, 4096], P('dp', 'mp'), may hold values from -1 to 2.5, as said below
- right_root: bfloat16 [1536, 4096], P('dp', 'mp'), may hold values from -1 to 2.5, as said below
Outputs:
- direction: bfloat16 [1536, 4096], P(None, 'mp')
- left_updated: float32 [1536, 4096], P('dp', 'mp')
- right_updated: float32 [1536, 4096], P('dp', 'mp')
Inputs may be any that keep to these rules, and one draw needn't show every extreme that they name: `band_owner`: a permutation: every index of dp owns exactly one band. `left_root`: in band order, every 512 x 512 block is symmetric. `right_root`: in band order, every 512 x 512 block is symmetric.
All inputs are finite; a program needn't handle non-finite values.
Results may differ from a plain program's by a relative error of at most 0.01.
Values may be sent and summed in bfloat16 or wider, within the bound.
A program may use at most 32 MiB of HBM per device.

v0:
```python
import jax
import jax.numpy as jnp
from jax import lax
from jax.sharding import PartitionSpec as P

BETA = 0.95


def against(band_rows, whole_rows, select):
    nblocks = select.shape[1]
    breadth = whole_rows.shape[1]
    blocks = whole_rows.reshape(nblocks, breadth, breadth)
    products = jnp.einsum("rk,bck->rbc", band_rows, blocks, preferred_element_type=jnp.float32)
    return jnp.sum(select[:, :, None] * products, axis=1)


def to_band_order(gathered, owners, members):
    shaped = gathered.reshape(members, -1, gathered.shape[1])
    return jnp.take(shaped, owners, axis=0).reshape(gathered.shape)


def shards(partial_grads, band_owner, left_factor, right_factor, left_root, right_root):
    members = lax.axis_size("dp")
    band_size = left_factor.shape[0]
    breadth = left_factor.shape[1]
    stacked = partial_grads.shape[1]
    nblocks = stacked // breadth
    devices = jnp.arange(members, dtype=jnp.int32)
    inverse = jnp.sum(
        jnp.where(band_owner[None, :] == devices[:, None], devices[None, :], 0), axis=1
    )
    own_band = inverse[lax.axis_index("dp")]
    partial_value = partial_grads[0]
    even_rows = lax.psum_scatter(
        partial_value.astype(jnp.float32), "dp", scatter_dimension=0, tiled=True
    ).astype(jnp.bfloat16)
    grad_full = lax.all_gather(even_rows, "dp", axis=0, tiled=True)
    grad_rows = lax.dynamic_slice_in_dim(grad_full, own_band * band_size, band_size, 0)
    global_rows = own_band * band_size + jnp.arange(band_size, dtype=jnp.int32)
    block_ids = global_rows // breadth
    within = global_rows % breadth
    block_range = jnp.arange(nblocks, dtype=jnp.int32)
    select = (block_ids[:, None] == block_range[None, :]).astype(jnp.float32)
    left_term = against(grad_rows, grad_full, select)
    left_updated = BETA * left_factor + (1.0 - BETA) * left_term
    column_range = jnp.arange(breadth, dtype=jnp.int32)
    onehot = (
        (block_range[:, None, None] == block_ids[None, None, :])
        & (column_range[None, :, None] == within[None, None, :])
    ).astype(jnp.bfloat16)
    blocks = grad_full.reshape(nblocks, breadth, breadth)
    columns = jnp.einsum("bkc,bcr->kr", blocks, onehot, preferred_element_type=jnp.float32).astype(
        jnp.bfloat16
    )
    right_products = jnp.einsum("kr,bkc->rbc", columns, blocks, preferred_element_type=jnp.float32)
    right_term = jnp.sum(select[:, :, None] * right_products, axis=1)
    right_updated = BETA * right_factor + (1.0 - BETA) * right_term
    mixed_rows = against(right_root, grad_full, select).astype(jnp.bfloat16)
    mixed_full = to_band_order(
        lax.all_gather(mixed_rows, "dp", axis=0, tiled=True), band_owner, members
    )
    direction_rows = against(left_root, mixed_full, select).astype(jnp.bfloat16)
    direction = to_band_order(
        lax.all_gather(direction_rows, "dp", axis=0, tiled=True), band_owner, members
    )
    return (direction, left_updated, right_updated)


def solution(mesh):
    placed = (P("dp", None, "mp"), P(), P("dp", "mp"), P("dp", "mp"), P("dp", "mp"), P("dp", "mp"))
    return jax.shard_map(
        shards,
        mesh=mesh,
        in_specs=placed,
        out_specs=(P(None, "mp"), P("dp", "mp"), P("dp", "mp")),
        check_vma=False,
    )
```

profile of v0, /device:TPU:1, one launch (start us, length us, event | category | flops | bytes accessed | tf_op | source)
XLA Modules:
  0.0 595.6 jit_solution(12395795141309368099)
XLA Ops:
  7.2 0.0 reduce-scatter.2.cloned.1.call-start
  7.2 3.5 bitcast_convert_fusion
  10.7 0.0 reduce-scatter.2.cloned.1.call-update
  10.8 0.0 all-gather.4.cloned.1.call-start
  10.8 214.7 %reduce-scatter.2.cloned.1.call-done = f32[16,512]{1,0:T(8,128)} async-done(((f32[1536,512]{1,0:T(8,128)}), f32[16,512]{1,0:T(8,128)}) %reduce-scatter.2.cloned.1.call-update) | async-done | bytes 32784 | tf_op jit(solution)/shard_map/reduce_scatter | solution.py:34
  225.5 1.4 convert_element_type.30
  226.9 0.0 all-gather.6.cloned.1.call-start
  227.0 0.1 select_reduce_fusion
  227.1 0.6 dynamic_slice.6
  228.4 123.7 %all-gather.4.cloned.1.call-done = bf16[1536,512]{1,0:T(8,128)(2,1)} async-done(((bf16[16,512]{1,0:T(8,128)(2,1)}), bf16[1536,512]{1,0:T(8,128)(2,1)}) %all-gather.4.cloned.1.call-update) | async-done | bytes 1572880 | tf_op jit(solution)/shard_map/all_gather | solution.py:37
  352.0 2.5 fusion.1
  354.6 0.0 all-gather.8.cloned.1.call-start
  354.7 114.2 %all-gather.6.cloned.1.call-done = bf16[1536,512]{1,0:T(8,128)(2,1)} async-done(((bf16[16,512]{1,0:T(8,128)(2,1)}), bf16[1536,512]{1,0:T(8,128)(2,1)}) %all-gather.6.cloned.1.call-update) | async-done | bytes 1572880 | tf_op jit(solution)/shard_map/all_gather | solution.py:60
  468.9 2.1 gather_fusion
  471.0 0.2 broadcast_select_fusion
  471.3 0.5 copy-done.4
  471.7 1.1 fusion.4
  473.0 0.5 fusion.2
  473.5 0.6 multiply_add_fusion.1
  474.1 0.8 fusion.3
  474.9 0.6 multiply_add_fusion
  475.6 110.0 %all-gather.8.cloned.1.call-done = bf16[1536,512]{1,0:T(8,128)(2,1)} async-done(((bf16[16,512]{1,0:T(8,128)(2,1)}), bf16[1536,512]{1,0:T(8,128)(2,1)}) %all-gather.8.cloned.1.call-update) | async-done | bytes 1572880 | tf_op jit(solution)/shard_map/all_gather | solution.py:64
  585.6 2.1 gather_fusion.1
  587.8 1.4 broadcast_select_fusion.1
  (21 shorter events, 0.2 us)
Async XLA Ops:
  7.2 344.9 %copy-start = (bf16[16,512]{1,0:T(8,128)(2,1)S(1)}, bf16[16,512]{1,0:T(8,128)(2,1)}, u32[]{:S(2)}) copy-start(bf16[16,512]{1,0:T(8,128)(2,1)} %param.13) | copy-start | bytes 49156
  7.2 218.3 %reduce-scatter.2.cloned.1.call-start = ((), (), s32[]{:S(2)}) async-start(), calls=%async_computation.1 | async-start | bytes 3178496 | tf_op jit(solution)/shard_map/reduce_scatter | solution.py:34
  10.7 216.2 %copy-start.5 = (s32[96]{0:T(128)S(1)}, s32[96]{0:T(128)}, u32[]{:S(2)}) copy-start(s32[96]{0:T(128)} %param.9) | copy-start | bytes 1156
  10.8 341.3 %all-gather.4.cloned.1.call-start = ((), (), s32[]{:S(2)}) async-start(), calls=%async_computation.2 | async-start | bytes 1589248 | tf_op jit(solution)/shard_map/all_gather | solution.py:37
  226.9 242.0 %all-gather.6.cloned.1.call-start = ((), (), s32[]{:S(2)}) async-start(), calls=%async_computation.3 | async-start | bytes 1589248 | tf_op jit(solution)/shard_map/all_gather | solution.py:60
  354.6 231.0 %all-gather.8.cloned.1.call-start = ((), (), s32[]{:S(2)}) async-start(), calls=%async_computation.4 | async-start | bytes 1589248 | tf_op jit(solution)/shard_map/all_gather | solution.py:64
  471.0 0.7 copy-start.4
  471.3 1.7 copy-start.1
  471.7 1.8 copy-start.2
  474.1 0.8 copy-start.3
Sparse Core Ops, SparseCore 0:
  13.3 212.2 reduce-scatter.1
  229.8 122.2 all-gather.3
  356.3 112.5 all-gather.5
  473.0 112.5 all-gather.7
where the time goes:
time: 596 us
  waiting for transfers between devices  563 us (94%)
  between operations  14.6 us (2%)
  other arithmetic  7.93 us (1%)
    reduce_scatter x1, waiting for transfers between devices, shards(): lax.psum_scatter(partial_value.astype(jnp.float32), 'dp', scatter_dimensi...  215 us
    all_gather x1, waiting for transfers between devices, shards(): grad_full = lax.all_gather(even_rows, 'dp', axis=0, tiled=True)  124 us
    all_gather x1, waiting for transfers between devices, shards(): lax.all_gather(mixed_rows, 'dp', axis=0, tiled=True)  114 us
    all_gather x1, waiting for transfers between devices, shards(): lax.all_gather(direction_rows, 'dp', axis=0, tiled=True)  110 us
  transfers between devices with their start and end apart: 4, of which 4 were waited for; matrix products, arithmetic and copies ran while one was open for 1% of the time, Pallas kernels for 0%

commit v1 on v0

v1 whole, which is shorter than its diff:
```python
import functools

import jax
import jax.numpy as jnp
from jax import lax
from jax.experimental import pallas as pl
from jax.experimental.pallas import tpu as pltpu
from jax.sharding import PartitionSpec as P

BETA = 0.95
NZ, NX, NC = 12, 4, 2
BAND = 16
BLK = 512
NB = 3
ROWS = NB * BLK
HALF = ROWS // NC
QUARTER = HALF // NX
EIGHTH = QUARTER // 2
MESH = pl.DeviceIdType.MESH
F32 = jnp.float32
BF16 = jnp.bfloat16
NEAR = [1, 11, 2, 10, 3, 9, 4, 8, 5, 7, 6]


def exchange(
    grad, left, right, g, p,
    r0, sb, ra, rb, rl, rr, qf, qb, rz, s1, s3,
    sem_local, c_send, c_recv, x_send, x_recv, z_send, z_recv,
    gz_send, gz_recv, gx_send, gx_recv, gc_send, gc_recv,
    px_send, px_recv, pz_send, pz_recv, pc_send, pc_recv,
):
    me = lax.axis_index("dp")
    c = lax.rem(me, NC)
    x = lax.rem(me // NC, NX)
    z = me // (NC * NX)

    def at(zz, xx, cc):
        return (zz * NX + xx) * NC + cc

    def up_x(k):
        return lax.rem(x + k, NX)

    def up_z(k):
        return lax.rem(z + k, NZ)

    partner = at(z, x, 1 - c)
    xp, xm = at(z, up_x(1), c), at(z, up_x(3), c)
    zp, zm = at(up_z(1), x, c), at(up_z(NZ - 1), x, c)
    pending = []

    def copy(src, dst, ss, rs, dev):
        return pltpu.make_async_remote_copy(
            src_ref=src, dst_ref=dst, send_sem=ss, recv_sem=rs,
            device_id={"dp": dev}, device_id_type=MESH,
        )

    def send(*args):
        made = copy(*args)
        made.start()
        pending.append(made)

    def arrived(dst, ss, rs, dev):
        copy(dst, dst, ss, rs, dev).wait_recv()

    barrier = pltpu.get_barrier_semaphore()
    others = [partner] + [at(z, up_x(k), c) for k in (1, 2, 3)]
    others += [at(up_z(k), x, c) for k in NEAR]
    for dev in others:
        pl.semaphore_signal(barrier, inc=1, device_id={"dp": dev}, device_id_type=MESH)

    slot = p.at[c, z, x]
    own = [
        pltpu.make_async_copy(left, slot.at[0], sem_local.at[0]),
        pltpu.make_async_copy(right, slot.at[1], sem_local.at[1]),
    ]
    for one in own:
        one.start()
    for one in own:
        one.wait()
    pl.semaphore_wait(barrier, len(others))

    def rows(start, size):
        return pl.ds(pl.multiple_of(start, BAND), size)

    for r in (2, 1, 3, 0):
        send(
            grad.at[0, rows((1 - c) * HALF + up_x(r) * QUARTER, QUARTER)],
            r0.at[r], c_send.at[r], c_recv.at[r], partner,
        )
    for k in (1, 2, 3):
        send(slot, slot, px_send.at[k], px_recv.at[k], at(z, up_x(k), c))

    def pair_sum(r):
        arrived(r0.at[r], c_send.at[r], c_recv.at[r], partner)
        mine = grad[0, rows(c * HALF + up_x(r) * QUARTER, QUARTER), :].astype(F32)
        return mine + r0[r].astype(F32)

    lo, hi = pl.ds(0, EIGHTH), pl.ds(EIGHTH, EIGHTH)
    sb[2] = pair_sum(2).astype(BF16)
    send(sb.at[2, lo], ra, x_send.at[0], x_recv.at[0], xp)
    send(sb.at[2, hi], rb, x_send.at[1], x_recv.at[1], xm)
    total = pair_sum(1)
    s1[...] = total[:EIGHTH]
    sb[1, hi] = total[EIGHTH:].astype(BF16)
    send(sb.at[1, hi], rl.at[hi], x_send.at[2], x_recv.at[2], xp)
    total = pair_sum(3)
    s3[...] = total[EIGHTH:]
    sb[3, lo] = total[:EIGHTH].astype(BF16)
    send(sb.at[3, lo], rr.at[lo], x_send.at[3], x_recv.at[3], xm)
    qf[...] = pair_sum(0)

    for k in (1, 2, 3):
        there = p.at[c, z, up_x(NX - k)]
        arrived(there, px_send.at[k], px_recv.at[k], xp)

    def plane(zz):
        return p.at[c, zz]

    def bands_on(step):
        if step > 1:
            for way, from_z in ((0, up_z(NZ + 1 - step)), (1, up_z(step - 1))):
                arrived(plane(from_z), pz_send.at[way, step - 1], pz_recv.at[way, step - 1], zp)
        if step <= 6:
            send(plane(up_z(NZ + 1 - step)), plane(up_z(NZ + 1 - step)),
                 pz_send.at[0, step], pz_recv.at[0, step], zp)
        if step <= 5:
            send(plane(up_z(step - 1)), plane(up_z(step - 1)),
                 pz_send.at[1, step], pz_recv.at[1, step], zm)
        for way, from_z in ((0, up_z(NZ + 1 - step)), (1, up_z(step - 1))):
            if way == 0 or step > 1:
                send(plane(from_z), plane(from_z),
                     pc_send.at[way, step], pc_recv.at[way, step], partner)

    bands_on(1)

    arrived(ra, x_send.at[0], x_recv.at[0], xm)
    sb[1, lo] = (s1[...] + ra[...].astype(F32)).astype(BF16)
    send(sb.at[1, lo], rl.at[lo], x_send.at[4], x_recv.at[4], xp)
    arrived(rb, x_send.at[1], x_recv.at[1], xp)
    sb[3, hi] = (s3[...] + rb[...].astype(F32)).astype(BF16)
    send(sb.at[3, hi], rr.at[hi], x_send.at[5], x_recv.at[5], xm)

    bands_on(2)

    arrived(rl.at[hi], x_send.at[2], x_recv.at[2], xm)
    arrived(rr.at[lo], x_send.at[3], x_recv.at[3], xp)
    arrived(rl.at[lo], x_send.at[4], x_recv.at[4], xm)
    arrived(rr.at[hi], x_send.at[5], x_recv.at[5], xp)
    total = qf[...] + rl[...].astype(F32) + rr[...].astype(F32)
    qf[...] = total
    qb[...] = total.astype(BF16)

    for d in reversed(NEAR):
        send(qb.at[rows(up_z(d) * BAND, BAND)], rz.at[d], z_send.at[d], z_recv.at[d],
             at(up_z(d), x, c))

    bands_on(3)

    for d in NEAR:
        arrived(rz.at[d], z_send.at[d], z_recv.at[d], zm)
    total = qf[rows(z * BAND, BAND), :]
    for d in NEAR:
        total = total + rz[d].astype(F32)

    def chunk(xx, zz):
        return g.at[rows((c * NX * NZ + xx * NZ + zz) * BAND, BAND)]

    g[rows((c * NX * NZ + x * NZ + z) * BAND, BAND), :] = total.astype(BF16)

    for d in reversed(NEAR):
        send(chunk(x, z), chunk(x, z), gz_send.at[d], gz_recv.at[d], at(up_z(d), x, c))

    bands_on(4)

    def from_z(d):
        return up_z(NZ - d)

    order = [0] + NEAR
    lag = 3
    for i in range(NZ + lag):
        if i < NZ:
            d = order[i]
            here = chunk(x, from_z(d))
            if d:
                arrived(here, gz_send.at[d], gz_recv.at[d], zm)
            send(here, here, gx_send.at[0, d], gx_recv.at[0, d], xp)
            send(here, here, gx_send.at[1, d], gx_recv.at[1, d], xm)
        if i == NZ - 1:
            mine = g.at[rows((c * NX + x) * QUARTER, QUARTER)]
            send(mine, mine, gc_send.at[0], gc_recv.at[0], partner)
        if i >= lag:
            d = order[i - lag]
            below, above = chunk(up_x(3), from_z(d)), chunk(up_x(1), from_z(d))
            arrived(below, gx_send.at[0, d], gx_recv.at[0, d], xm)
            if d % 2 == 0:
                send(below, below, gx_send.at[2, d], gx_recv.at[2, d], xp)
            arrived(above, gx_send.at[1, d], gx_recv.at[1, d], xp)
            if d % 2 == 1:
                send(above, above, gx_send.at[2, d], gx_recv.at[2, d], xm)
        if i == 5:
            bands_on(5)
        if i == 11:
            bands_on(6)
    for k, r in ((1, 1), (2, 3)):
        part = g.at[rows((c * NX + up_x(r)) * QUARTER, QUARTER)]
        send(part, part, gc_send.at[k], gc_recv.at[k], partner)
    for d in order:
        arrived(chunk(up_x(2), from_z(d)), gx_send.at[2, d], gx_recv.at[2, d], xp)
    part = g.at[rows((c * NX + up_x(2)) * QUARTER, QUARTER)]
    send(part, part, gc_send.at[3], gc_recv.at[3], partner)

    last = plane(up_z(6))
    arrived(last, pz_send.at[0, 6], pz_recv.at[0, 6], zm)
    send(last, last, pc_send.at[0, 7], pc_recv.at[0, 7], partner)

    for k, r in ((0, 0), (1, 1), (2, 3), (3, 2)):
        part = g.at[rows(((1 - c) * NX + up_x(r)) * QUARTER, QUARTER)]
        arrived(part, gc_send.at[k], gc_recv.at[k], partner)
    for step in range(1, 8):
        for way, zz in ((0, up_z(NZ + 1 - step)), (1, up_z(step - 1))):
            if (way == 0 or step > 1) and not (way == 1 and step == 7):
                arrived(p.at[1 - c, zz], pc_send.at[way, step], pc_recv.at[way, step], partner)
    for made in pending:
        made.wait_send()


def gather_all(grad, left, right):
    vmem = pl.BlockSpec(memory_space=pltpu.VMEM)
    dma = pltpu.SemaphoreType.DMA
    return pl.pallas_call(
        exchange,
        out_shape=(
            jax.ShapeDtypeStruct((ROWS, BLK), BF16),
            jax.ShapeDtypeStruct((NC, NZ, NX, 2, BAND, BLK), BF16),
        ),
        in_specs=[vmem] * 3,
        out_specs=(vmem, vmem),
        scratch_shapes=[
            pltpu.VMEM((NX, QUARTER, BLK), BF16),
            pltpu.VMEM((NX, QUARTER, BLK), BF16),
            pltpu.VMEM((EIGHTH, BLK), BF16),
            pltpu.VMEM((EIGHTH, BLK), BF16),
            pltpu.VMEM((QUARTER, BLK), BF16),
            pltpu.VMEM((QUARTER, BLK), BF16),
            pltpu.VMEM((QUARTER, BLK), F32),
            pltpu.VMEM((QUARTER, BLK), BF16),
            pltpu.VMEM((NZ, BAND, BLK), BF16),
            pltpu.VMEM((EIGHTH, BLK), F32),
            pltpu.VMEM((EIGHTH, BLK), F32),
            dma((2,)),
            dma((NX,)), dma((NX,)),
            dma((6,)), dma((6,)),
            dma((NZ,)), dma((NZ,)),
            dma((NZ,)), dma((NZ,)),
            dma((3, NZ)), dma((3, NZ)),
            dma((NX,)), dma((NX,)),
            dma((NX,)), dma((NX,)),
            dma((2, 7)), dma((2, 7)),
            dma((2, 8)), dma((2, 8)),
        ],
        compiler_params=pltpu.CompilerParams(
            collective_id=0, has_side_effects=True, vmem_limit_bytes=40 << 20
        ),
    )(grad, left, right)


def dots(owner, g, p, left_factor, right_factor, direction, left_out, right_out, pls, prs):
    me = lax.axis_index("dp")

    def place(k, own):
        d = owner[k]
        cc, xx, zz = lax.rem(d, NC), lax.rem(d // NC, NX), d // (NC * NX)
        at = pl.ds(pl.multiple_of(k * BAND, BAND), BAND)
        pls[at, :] = p[cc, zz, xx, 0]
        prs[at, :] = p[cc, zz, xx, 1]
        return jnp.where(d == me, k, own)

    own = lax.fori_loop(0, NZ * NX * NC, place, jnp.int32(0), unroll=8)
    start = own * BAND
    block = start // BLK
    within = start - block * BLK
    row = g[pl.ds(pl.multiple_of(start, BAND), BAND), :]
    gb = g[pl.ds(pl.multiple_of(block * BLK, BLK), BLK), :]
    last = (((1,), (1,)), ((), ()))
    left_term = lax.dot_general(row, gb, last, preferred_element_type=F32)
    left_out[...] = BETA * left_factor[...] + (1.0 - BETA) * left_term
    which = lax.broadcasted_iota(jnp.int32, (BAND, BLK), 1)
    this = lax.broadcasted_iota(jnp.int32, (BAND, BLK), 0) + within
    onehot = jnp.where(which == this, 1.0, 0.0).astype(BF16)
    column = lax.dot_general(onehot, gb, last, preferred_element_type=F32).astype(BF16)
    right_term = jnp.dot(column, gb, preferred_element_type=F32)
    right_out[...] = BETA * right_factor[...] + (1.0 - BETA) * right_term
    for b in range(NB):
        at = pl.ds(b * BLK, BLK)
        mixed = jnp.dot(g[at, :], prs[at, :], preferred_element_type=F32).astype(BF16)
        direction[at, :] = jnp.dot(pls[at, :], mixed, preferred_element_type=F32).astype(BF16)


def precondition(owner, g, p, left_factor, right_factor):
    vmem = pl.BlockSpec(memory_space=pltpu.VMEM)
    return pl.pallas_call(
        dots,
        out_shape=(
            jax.ShapeDtypeStruct((ROWS, BLK), BF16),
            jax.ShapeDtypeStruct((BAND, BLK), F32),
            jax.ShapeDtypeStruct((BAND, BLK), F32),
        ),
        in_specs=[pl.BlockSpec(memory_space=pltpu.SMEM)] + [vmem] * 4,
        out_specs=(vmem, vmem, vmem),
        scratch_shapes=[pltpu.VMEM((ROWS, BLK), BF16), pltpu.VMEM((ROWS, BLK), BF16)],
        compiler_params=pltpu.CompilerParams(vmem_limit_bytes=40 << 20),
    )(owner, g, p, left_factor, right_factor)


def shards(partial_grads, band_owner, left_factor, right_factor, left_root, right_root):
    g, p = gather_all(partial_grads, left_root, right_root)
    return precondition(band_owner, g, p, left_factor, right_factor)


def solution(mesh):
    placed = (P("dp", None, "mp"), P(), P("dp", "mp"), P("dp", "mp"), P("dp", "mp"), P("dp", "mp"))
    return jax.shard_map(
        shards,
        mesh=mesh,
        in_specs=placed,
        out_specs=(P(None, "mp"), P("dp", "mp"), P("dp", "mp")),
        check_vma=False,
    )
```

time: 596 us -> 74.3 us (0.12)
  waiting for transfers between devices: 563 us -> 0 us
  Pallas kernels: 0 us -> 70.5 us
  between operations: 14.6 us -> 0.68 us
  other arithmetic: 7.93 us -> 0 us
    all_gather x3 -> x0, waiting for transfers between devices: 348 us -> none  [the longest x1 124 us: shards(): grad_full = lax.all_gather(even_rows, 'dp', axis=0, tiled=True)]
    reduce_scatter x1 -> x0, waiting for transfers between devices: 215 us -> none  [shards(): lax.psum_scatter(partial_value.astype(jnp.float32), 'dp', scatter_dimensi...]
    pallas_call x0 -> x2, Pallas kernels: none -> 70.5 us  [the longest x1 64.9 us: gather_all(): pl.pallas_call(exchange, out_shape=(jax.ShapeDtypeStruct((ROWS, BLK), BF1...]
  transfers between devices with their start and end apart: 4 -> 0, of which waited for: 4 -> 0; matrix products, arithmetic and copies ran while one was open for 1% -> 0% of each run, Pallas kernels for 0% -> 0%
where the time goes in v1:
time: 74.3 us; the launch traced here: 74 us
  Pallas kernels  70.5 us (95%)
  local copies, waits for them, and re-layouts  2.85 us (4%)
    pallas_call x1, Pallas kernels, gather_all(): pl.pallas_call(exchange, out_shape=(jax.ShapeDtypeStruct((ROWS, BLK), BF1...  64.9 us
    pallas_call x1, Pallas kernels, precondition(): pl.pallas_call(dots, out_shape=(jax.ShapeDtypeStruct((ROWS, BLK), BF16),...  5.53 us
    unnamed x12, local copies, waits for them, and re-layouts  2.85 us

profile of v1, /device:TPU:1, one launch (start us, length us, event | category | flops | bytes accessed | tf_op | source)
XLA Modules:
  0.0 74.0 jit_solution(9537672814476022099)
XLA Ops:
  0.6 0.0 copy-start
  0.6 1.4 %copy-done = bf16[1,1536,512]{2,1,0:T(8,128)(2,1)S(1)} copy-done((bf16[1,1536,512]{2,1,0:T(8,128)(2,1)S(1)}, bf16[1,1536,512]{2,1,0:T(8,128)(2,1)}, u32[]{:S(2)}) %copy-start) | copy-done | bytes 1572888
  2.0 0.0 copy-start.3
  2.0 0.7 copy-done.3
  2.8 0.0 copy-start.4
  2.8 0.7 copy-done.4
  3.5 0.0 copy-start.1
  3.5 0.0 copy-start.2
  3.5 0.0 copy-start.5
  3.5 64.9 %shard_map.85 = (bf16[1536,512]{1,0:T(8,128)(2,1)S(1)}, bf16[2,12,4,2,16,512]{5,4,3,2,1,0:T(8,128)(2,1)S(1)}) custom-call(bf16[1,1536,512]{2,1,0:T(8,128)(2,1)S(1)} %copy-done, bf16[16,512]{1,0:T(8,128)(2,1)S(1)} %copy-done.3, bf16[16,512]{1,0:T(8,128)(2,1)S(1)} %copy-done.4), custom_call_target="tpu_custom_call" | custom-call | tf_op jit(solution)/shard_map/pallas_call | solution.py:230
  68.4 0.0 copy-done.1
  68.4 0.0 copy-done.2
  68.4 0.0 copy-done.5
  68.4 5.5 %shard_map.86 = (bf16[1536,512]{1,0:T(8,128)(2,1)}, f32[16,512]{1,0:T(8,128)}, f32[16,512]{1,0:T(8,128)}) custom-call(s32[96]{0:T(128)S(1)} %copy-done.5, bf16[1536,512]{1,0:T(8,128)(2,1)S(1)} %get-tuple-element.5.g, bf16[2,12,4,2,16,512]{5,4,3,2,1,0:T(8,128)(2,1)S(1)} %get-tuple-element.6.p, f32[16,512]{1,0:T(8,128)S(1)} %copy-done.1, f32[16,512]{1,0:T(8,128)S(1)} %copy-done.2), custom_call_target="tpu_custom_call" | custom-call | tf_op jit(solution)/shard_map/pallas_call | solution.py:301
Async XLA Ops:
  0.6 1.4 %copy-start = (bf16[1,1536,512]{2,1,0:T(8,128)(2,1)S(1)}, bf16[1,1536,512]{2,1,0:T(8,128)(2,1)}, u32[]{:S(2)}) copy-start(bf16[1,1536,512]{2,1,0:T(8,128)(2,1)} %grad.1) | copy-start | bytes 4718596
  2.0 0.7 copy-start.3
  2.8 0.7 copy-start.4
  3.5 64.9 %copy-start.1 = (f32[16,512]{1,0:T(8,128)S(1)}, f32[16,512]{1,0:T(8,128)}, u32[]{:S(2)}) copy-start(f32[16,512]{1,0:T(8,128)} %left_factor.1) | copy-start | bytes 98308
  3.5 64.9 %copy-start.2 = (f32[16,512]{1,0:T(8,128)S(1)}, f32[16,512]{1,0:T(8,128)}, u32[]{:S(2)}) copy-start(f32[16,512]{1,0:T(8,128)} %right_factor.1) | copy-start | bytes 98308
  3.5 65.0 %copy-start.5 = (s32[96]{0:T(128)S(1)}, s32[96]{0:T(128)}, u32[]{:S(2)}) copy-start(s32[96]{0:T(128)} %owner.1) | copy-start | bytes 1156

commit v2 on v1

--- a/solution.py
+++ b/solution.py
@@ -24,7 +24,7 @@
 
 def exchange(
     grad, left, right, g, p,
-    r0, sb, ra, rb, rl, rr, qf, qb, rz, s1, s3,
+    half, r0, sb, ra, rb, rl, rr, qf, qb, rz, s1, s3,
     sem_local, c_send, c_recv, x_send, x_recv, z_send, z_recv,
     gz_send, gz_recv, gx_send, gx_recv, gc_send, gc_recv,
     px_send, px_recv, pz_send, pz_recv, pc_send, pc_recv,
@@ -68,32 +68,38 @@
     for dev in others:
         pl.semaphore_signal(barrier, inc=1, device_id={"dp": dev}, device_id_type=MESH)
 
-    slot = p.at[c, z, x]
+    def rows(start, size):
+        return pl.ds(pl.multiple_of(start, BAND), size)
+
+    slot = p.at[c, x, z]
     own = [
         pltpu.make_async_copy(left, slot.at[0], sem_local.at[0]),
         pltpu.make_async_copy(right, slot.at[1], sem_local.at[1]),
     ]
-    for one in own:
+    loads = {
+        r: pltpu.make_async_copy(
+            grad.at[0, rows(c * HALF + up_x(r) * QUARTER, QUARTER)], half.at[r], sem_local.at[2 + r]
+        )
+        for r in (2, 1, 3, 0)
+    }
+    for one in own + list(loads.values()):
         one.start()
-    for one in own:
-        one.wait()
     pl.semaphore_wait(barrier, len(others))
-
-    def rows(start, size):
-        return pl.ds(pl.multiple_of(start, BAND), size)
 
     for r in (2, 1, 3, 0):
         send(
             grad.at[0, rows((1 - c) * HALF + up_x(r) * QUARTER, QUARTER)],
             r0.at[r], c_send.at[r], c_recv.at[r], partner,
         )
-    for k in (1, 2, 3):
-        send(slot, slot, px_send.at[k], px_recv.at[k], at(z, up_x(k), c))
+    for one in own:
+        one.wait()
+    for d in reversed(NEAR):
+        send(slot, slot, pz_send.at[d], pz_recv.at[d], at(up_z(d), x, c))
 
     def pair_sum(r):
+        loads[r].wait()
         arrived(r0.at[r], c_send.at[r], c_recv.at[r], partner)
-        mine = grad[0, rows(c * HALF + up_x(r) * QUARTER, QUARTER), :].astype(F32)
-        return mine + r0[r].astype(F32)
+        return half[r].astype(F32) + r0[r].astype(F32)
 
     lo, hi = pl.ds(0, EIGHTH), pl.ds(EIGHTH, EIGHTH)
     sb[2] = pair_sum(2).astype(BF16)
@@ -109,30 +115,6 @@
     send(sb.at[3, lo], rr.at[lo], x_send.at[3], x_recv.at[3], xm)
     qf[...] = pair_sum(0)
 
-    for k in (1, 2, 3):
-        there = p.at[c, z, up_x(NX - k)]
-        arrived(there, px_send.at[k], px_recv.at[k], xp)
-
-    def plane(zz):
-        return p.at[c, zz]
-
-    def bands_on(step):
-        if step > 1:
-            for way, from_z in ((0, up_z(NZ + 1 - step)), (1, up_z(step - 1))):
-                arrived(plane(from_z), pz_send.at[way, step - 1], pz_recv.at[way, step - 1], zp)
-        if step <= 6:
-            send(plane(up_z(NZ + 1 - step)), plane(up_z(NZ + 1 - step)),
-                 pz_send.at[0, step], pz_recv.at[0, step], zp)
-        if step <= 5:
-            send(plane(up_z(step - 1)), plane(up_z(step - 1)),
-                 pz_send.at[1, step], pz_recv.at[1, step], zm)
-        for way, from_z in ((0, up_z(NZ + 1 - step)), (1, up_z(step - 1))):
-            if way == 0 or step > 1:
-                send(plane(from_z), plane(from_z),
-                     pc_send.at[way, step], pc_recv.at[way, step], partner)
-
-    bands_on(1)
-
     arrived(ra, x_send.at[0], x_recv.at[0], xm)
     sb[1, lo] = (s1[...] + ra[...].astype(F32)).astype(BF16)
     send(sb.at[1, lo], rl.at[lo], x_send.at[4], x_recv.at[4], xp)
@@ -140,7 +122,6 @@
     sb[3, hi] = (s3[...] + rb[...].astype(F32)).astype(BF16)
     send(sb.at[3, hi], rr.at[hi], x_send.at[5], x_recv.at[5], xm)
 
-    bands_on(2)
 
     arrived(rl.at[hi], x_send.at[2], x_recv.at[2], xm)
     arrived(rr.at[lo], x_send.at[3], x_recv.at[3], xp)
@@ -154,7 +135,26 @@
         send(qb.at[rows(up_z(d) * BAND, BAND)], rz.at[d], z_send.at[d], z_recv.at[d],
              at(up_z(d), x, c))
 
-    bands_on(3)
+
+    def from_z(d):
+        return up_z(NZ - d)
+
+    def bands(r, k=None):
+        return p.at[c, up_x(r)] if k is None else p.at[c, up_x(r), pl.ds(k * (NZ // 2), NZ // 2)]
+
+    def pass_bands(r, k, i, dev):
+        send(bands(r, k), bands(r, k), px_send.at[i, k], px_recv.at[i, k], dev)
+
+    def give_bands(r, i):
+        send(bands(r), bands(r), pc_send.at[i], pc_recv.at[i], partner)
+
+    for d in NEAR:
+        arrived(p.at[c, x, from_z(d)], pz_send.at[d], pz_recv.at[d], zm)
+    pass_bands(0, 0, 0, xp)
+    pass_bands(0, 1, 1, xm)
+    pass_bands(0, 1, 0, xp)
+    pass_bands(0, 0, 1, xm)
+    give_bands(0, 0)
 
     for d in NEAR:
         arrived(rz.at[d], z_send.at[d], z_recv.at[d], zm)
@@ -167,59 +167,51 @@
 
     g[rows((c * NX * NZ + x * NZ + z) * BAND, BAND), :] = total.astype(BF16)
 
+    own_chunk = chunk(x, z)
     for d in reversed(NEAR):
-        send(chunk(x, z), chunk(x, z), gz_send.at[d], gz_recv.at[d], at(up_z(d), x, c))
-
-    bands_on(4)
-
-    def from_z(d):
-        return up_z(NZ - d)
-
-    order = [0] + NEAR
-    lag = 3
-    for i in range(NZ + lag):
-        if i < NZ:
-            d = order[i]
-            here = chunk(x, from_z(d))
-            if d:
-                arrived(here, gz_send.at[d], gz_recv.at[d], zm)
-            send(here, here, gx_send.at[0, d], gx_recv.at[0, d], xp)
-            send(here, here, gx_send.at[1, d], gx_recv.at[1, d], xm)
-        if i == NZ - 1:
-            mine = g.at[rows((c * NX + x) * QUARTER, QUARTER)]
-            send(mine, mine, gc_send.at[0], gc_recv.at[0], partner)
-        if i >= lag:
-            d = order[i - lag]
-            below, above = chunk(up_x(3), from_z(d)), chunk(up_x(1), from_z(d))
-            arrived(below, gx_send.at[0, d], gx_recv.at[0, d], xm)
-            if d % 2 == 0:
-                send(below, below, gx_send.at[2, d], gx_recv.at[2, d], xp)
-            arrived(above, gx_send.at[1, d], gx_recv.at[1, d], xp)
-            if d % 2 == 1:
-                send(above, above, gx_send.at[2, d], gx_recv.at[2, d], xm)
-        if i == 5:
-            bands_on(5)
-        if i == 11:
-            bands_on(6)
-    for k, r in ((1, 1), (2, 3)):
-        part = g.at[rows((c * NX + up_x(r)) * QUARTER, QUARTER)]
-        send(part, part, gc_send.at[k], gc_recv.at[k], partner)
-    for d in order:
-        arrived(chunk(up_x(2), from_z(d)), gx_send.at[2, d], gx_recv.at[2, d], xp)
-    part = g.at[rows((c * NX + up_x(2)) * QUARTER, QUARTER)]
-    send(part, part, gc_send.at[3], gc_recv.at[3], partner)
-
-    last = plane(up_z(6))
-    arrived(last, pz_send.at[0, 6], pz_recv.at[0, 6], zm)
-    send(last, last, pc_send.at[0, 7], pc_recv.at[0, 7], partner)
-
-    for k, r in ((0, 0), (1, 1), (2, 3), (3, 2)):
-        part = g.at[rows(((1 - c) * NX + up_x(r)) * QUARTER, QUARTER)]
-        arrived(part, gc_send.at[k], gc_recv.at[k], partner)
-    for step in range(1, 8):
-        for way, zz in ((0, up_z(NZ + 1 - step)), (1, up_z(step - 1))):
-            if (way == 0 or step > 1) and not (way == 1 and step == 7):
-                arrived(p.at[1 - c, zz], pc_send.at[way, step], pc_recv.at[way, step], partner)
+        send(own_chunk, own_chunk, gz_send.at[d], gz_recv.at[d], at(up_z(d), x, c))
+    arrived(bands(3, 0), px_send.at[0, 0], px_recv.at[0, 0], xm)
+    pass_bands(3, 0, 2, xp)
+    arrived(bands(1, 1), px_send.at[1, 1], px_recv.at[1, 1], xp)
+    pass_bands(1, 1, 2, xm)
+    arrived(bands(3, 1), px_send.at[0, 1], px_recv.at[0, 1], xm)
+    give_bands(3, 1)
+    arrived(bands(1, 0), px_send.at[1, 0], px_recv.at[1, 0], xp)
+    give_bands(1, 2)
+    for d in NEAR:
+        arrived(chunk(x, from_z(d)), gz_send.at[d], gz_recv.at[d], zm)
+
+    arrived(bands(2, 0), px_send.at[2, 0], px_recv.at[2, 0], xm)
+    arrived(bands(2, 1), px_send.at[2, 1], px_recv.at[2, 1], xp)
+    give_bands(2, 3)
+    def part(r, a, n):
+        return g.at[rows((c * NX + up_x(r)) * QUARTER + a, n)]
+
+    mine = part(0, 0, QUARTER)
+    lo_half, hi_half = part(0, 0, EIGHTH), part(0, EIGHTH, EIGHTH)
+    send(lo_half, lo_half, gx_send.at[0, 0], gx_recv.at[0, 0], xp)
+    send(hi_half, hi_half, gx_send.at[1, 1], gx_recv.at[1, 1], xm)
+    send(hi_half, hi_half, gx_send.at[0, 1], gx_recv.at[0, 1], xp)
+    send(lo_half, lo_half, gx_send.at[1, 0], gx_recv.at[1, 0], xm)
+    send(mine, mine, gc_send.at[0, 0], gc_recv.at[0, 0], partner)
+    below, above = part(3, 0, EIGHTH), part(1, EIGHTH, EIGHTH)
+    arrived(below, gx_send.at[0, 0], gx_recv.at[0, 0], xm)
+    send(below, below, gx_send.at[2, 0], gx_recv.at[2, 0], xp)
+    arrived(above, gx_send.at[1, 1], gx_recv.at[1, 1], xp)
+    send(above, above, gx_send.at[2, 1], gx_recv.at[2, 1], xm)
+    arrived(part(3, EIGHTH, EIGHTH), gx_send.at[0, 1], gx_recv.at[0, 1], xm)
+    send(part(3, 0, QUARTER), part(3, 0, QUARTER), gc_send.at[1, 0], gc_recv.at[1, 0], partner)
+    arrived(part(1, 0, EIGHTH), gx_send.at[1, 0], gx_recv.at[1, 0], xp)
+    send(part(1, 0, QUARTER), part(1, 0, QUARTER), gc_send.at[2, 0], gc_recv.at[2, 0], partner)
+    arrived(part(2, 0, EIGHTH), gx_send.at[2, 0], gx_recv.at[2, 0], xm)
+    arrived(part(2, EIGHTH, EIGHTH), gx_send.at[2, 1], gx_recv.at[2, 1], xp)
+    send(part(2, 0, QUARTER), part(2, 0, QUARTER), gc_send.at[3, 0], gc_recv.at[3, 0], partner)
+
+    for k, r in ((0, 0), (1, 3), (2, 1), (3, 2)):
+        theirs = g.at[rows(((1 - c) * NX + up_x(r)) * QUARTER, QUARTER)]
+        arrived(theirs, gc_send.at[k, 0], gc_recv.at[k, 0], partner)
+    for i, r in ((0, 0), (1, 3), (2, 1), (3, 2)):
+        arrived(p.at[1 - c, up_x(r)], pc_send.at[i], pc_recv.at[i], partner)
     for made in pending:
         made.wait_send()
 
@@ -231,11 +223,12 @@
         exchange,
         out_shape=(
             jax.ShapeDtypeStruct((ROWS, BLK), BF16),
-            jax.ShapeDtypeStruct((NC, NZ, NX, 2, BAND, BLK), BF16),
+            jax.ShapeDtypeStruct((NC, NX, NZ, 2, BAND, BLK), BF16),
         ),
-        in_specs=[vmem] * 3,
+        in_specs=[pl.BlockSpec(memory_space=pltpu.HBM)] * 3,
         out_specs=(vmem, vmem),
         scratch_shapes=[
+            pltpu.VMEM((NX, QUARTER, BLK), BF16),
             pltpu.VMEM((NX, QUARTER, BLK), BF16),
             pltpu.VMEM((NX, QUARTER, BLK), BF16),
             pltpu.VMEM((EIGHTH, BLK), BF16),
@@ -247,16 +240,16 @@
             pltpu.VMEM((NZ, BAND, BLK), BF16),
             pltpu.VMEM((EIGHTH, BLK), F32),
             pltpu.VMEM((EIGHTH, BLK), F32),
-            dma((2,)),
+            dma((2 + NX,)),
             dma((NX,)), dma((NX,)),
             dma((6,)), dma((6,)),
             dma((NZ,)), dma((NZ,)),
             dma((NZ,)), dma((NZ,)),
             dma((3, NZ)), dma((3, NZ)),
+            dma((NX, NZ)), dma((NX, NZ)),
+            dma((3, 2)), dma((3, 2)),
+            dma((NZ,)), dma((NZ,)),
             dma((NX,)), dma((NX,)),
-            dma((NX,)), dma((NX,)),
-            dma((2, 7)), dma((2, 7)),
-            dma((2, 8)), dma((2, 8)),
         ],
         compiler_params=pltpu.CompilerParams(
             collective_id=0, has_side_effects=True, vmem_limit_bytes=40 << 20
@@ -271,8 +264,8 @@
         d = owner[k]
         cc, xx, zz = lax.rem(d, NC), lax.rem(d // NC, NX), d // (NC * NX)
         at = pl.ds(pl.multiple_of(k * BAND, BAND), BAND)
-        pls[at, :] = p[cc, zz, xx, 0]
-        prs[at, :] = p[cc, zz, xx, 1]
+        pls[at, :] = p[cc, xx, zz, 0]
+        prs[at, :] = p[cc, xx, zz, 1]
         return jnp.where(d == me, k, own)
 
     own = lax.fori_loop(0, NZ * NX * NC, place, jnp.int32(0), unroll=8)

time: 74.3 us -> 68.9 us (0.927)
  Pallas kernels: 70.5 us -> 65 us
    pallas_call x1, Pallas kernels: 64.9 us -> 59.5 us  [gather_all(): pl.pallas_call(exchange, out_shape=(jax.ShapeDtypeStruct((ROWS, BLK), BF1...]
where the time goes in v2:
time: 68.9 us; the launch traced here: 68.5 us
  Pallas kernels  65 us (94%)
  local copies, waits for them, and re-layouts  2.85 us (4%)
    pallas_call x1, Pallas kernels, gather_all(): pl.pallas_call(exchange, out_shape=(jax.ShapeDtypeStruct((ROWS, BLK), BF1...  59.5 us
    pallas_call x1, Pallas kernels, precondition(): pl.pallas_call(dots, out_shape=(jax.ShapeDtypeStruct((ROWS, BLK), BF16),...  5.55 us
    unnamed x12, local copies, waits for them, and re-layouts  2.85 us

profile of v2, /device:TPU:1, one launch (start us, length us, event | category | flops | bytes accessed | tf_op | source)
XLA Modules:
  0.0 68.5 jit_solution(10201897039147031084)
XLA Ops:
  0.6 0.0 copy-start
  0.6 1.4 %copy-done = bf16[1,1536,512]{2,1,0:T(8,128)(2,1)S(1)} copy-done((bf16[1,1536,512]{2,1,0:T(8,128)(2,1)S(1)}, bf16[1,1536,512]{2,1,0:T(8,128)(2,1)}, u32[]{:S(2)}) %copy-start) | copy-done | bytes 1572888
  2.0 0.0 copy-start.3
  2.0 0.7 %copy-done.3 = bf16[16,512]{1,0:T(8,128)(2,1)S(1)} copy-done((bf16[16,512]{1,0:T(8,128)(2,1)S(1)}, bf16[16,512]{1,0:T(8,128)(2,1)}, u32[]{:S(2)}) %copy-start.3) | copy-done | bytes 16408
  2.8 0.0 copy-start.4
  2.8 0.7 %copy-done.4 = bf16[16,512]{1,0:T(8,128)(2,1)S(1)} copy-done((bf16[16,512]{1,0:T(8,128)(2,1)S(1)}, bf16[16,512]{1,0:T(8,128)(2,1)}, u32[]{:S(2)}) %copy-start.4) | copy-done | bytes 16408
  3.5 0.0 copy-start.1
  3.5 0.0 copy-start.2
  3.5 0.0 copy-start.5
  3.5 59.5 %shard_map.85 = (bf16[1536,512]{1,0:T(8,128)(2,1)S(1)}, bf16[2,4,12,2,16,512]{5,4,3,2,1,0:T(8,128)(2,1)S(1)}) custom-call(bf16[1,1536,512]{2,1,0:T(8,128)(2,1)S(1)} %copy-done, bf16[16,512]{1,0:T(8,128)(2,1)S(1)} %copy-done.3, bf16[16,512]{1,0:T(8,128)(2,1)S(1)} %copy-done.4), custom_call_target="tpu_custom_call" | custom-call | tf_op jit(solution)/shard_map/pallas_call | solution.py:222
  63.0 0.0 copy-done.1
  63.0 0.0 copy-done.2
  63.0 0.0 copy-done.5
  63.0 5.5 %shard_map.86 = (bf16[1536,512]{1,0:T(8,128)(2,1)}, f32[16,512]{1,0:T(8,128)}, f32[16,512]{1,0:T(8,128)}) custom-call(s32[96]{0:T(128)S(1)} %copy-done.5, bf16[1536,512]{1,0:T(8,128)(2,1)S(1)} %get-tuple-element.5.g, bf16[2,4,12,2,16,512]{5,4,3,2,1,0:T(8,128)(2,1)S(1)} %get-tuple-element.6.p, f32[16,512]{1,0:T(8,128)S(1)} %copy-done.1, f32[16,512]{1,0:T(8,128)S(1)} %copy-done.2), custom_call_target="tpu_custom_call" | custom-call | tf_op jit(solution)/shard_map/pallas_call | solution.py:294
Async XLA Ops:
  0.6 1.4 %copy-start = (bf16[1,1536,512]{2,1,0:T(8,128)(2,1)S(1)}, bf16[1,1536,512]{2,1,0:T(8,128)(2,1)}, u32[]{:S(2)}) copy-start(bf16[1,1536,512]{2,1,0:T(8,128)(2,1)} %grad.1) | copy-start | bytes 4718596
  2.0 0.7 %copy-start.3 = (bf16[16,512]{1,0:T(8,128)(2,1)S(1)}, bf16[16,512]{1,0:T(8,128)(2,1)}, u32[]{:S(2)}) copy-start(bf16[16,512]{1,0:T(8,128)(2,1)} %left.1) | copy-start | bytes 49156
  2.8 0.7 %copy-start.4 = (bf16[16,512]{1,0:T(8,128)(2,1)S(1)}, bf16[16,512]{1,0:T(8,128)(2,1)}, u32[]{:S(2)}) copy-start(bf16[16,512]{1,0:T(8,128)(2,1)} %right.1) | copy-start | bytes 49156
  3.5 59.5 %copy-start.1 = (f32[16,512]{1,0:T(8,128)S(1)}, f32[16,512]{1,0:T(8,128)}, u32[]{:S(2)}) copy-start(f32[16,512]{1,0:T(8,128)} %left_factor.1) | copy-start | bytes 98308
  3.5 59.5 %copy-start.2 = (f32[16,512]{1,0:T(8,128)S(1)}, f32[16,512]{1,0:T(8,128)}, u32[]{:S(2)}) copy-start(f32[16,512]{1,0:T(8,128)} %right_factor.1) | copy-start | bytes 98308
  3.5 59.5 %copy-start.5 = (s32[96]{0:T(128)S(1)}, s32[96]{0:T(128)}, u32[]{:S(2)}) copy-start(s32[96]{0:T(128)} %owner.1) | copy-start | bytes 1156

commit v3 on v2

--- a/solution.py
+++ b/solution.py
@@ -23,8 +23,8 @@
 
 
 def exchange(
-    grad, left, right, g, p,
-    half, r0, sb, ra, rb, rl, rr, qf, qb, rz, s1, s3,
+    owner, grad, left, right, g, pls, prs,
+    p, half, r0, sb, ra, rb, rl, rr, qf, qb, rz, s1, s3,
     sem_local, c_send, c_recv, x_send, x_recv, z_send, z_recv,
     gz_send, gz_recv, gx_send, gx_recv, gc_send, gc_recv,
     px_send, px_recv, pz_send, pz_recv, pc_send, pc_recv,
@@ -93,51 +93,91 @@
         )
     for one in own:
         one.wait()
-    for d in reversed(NEAR):
-        send(slot, slot, pz_send.at[d], pz_recv.at[d], at(up_z(d), x, c))
-
-    def pair_sum(r):
+    def from_z(d):
+        return up_z(NZ - d)
+
+    def band_along(d, k):
+        band = p.at[c, x, from_z(d)]
+        to = (d + k) % NZ
+        send(band, band, pz_send.at[to], pz_recv.at[to], at(up_z(k % NZ), x, c))
+
+    for k in (3, -3, 2, -2, 1, -1):
+        band_along(0, k)
+
+    far = list(range(4, 9))
+    near = list(range(9, 12)) + list(range(0, 4))
+    far_lo, far_hi = pl.ds(0, 3 * BAND), pl.ds(3 * BAND, 2 * BAND)
+    near_lo, near_hi = pl.ds(5 * BAND, 4 * BAND), pl.ds(9 * BAND, 3 * BAND)
+    all_far, all_near = pl.ds(0, 5 * BAND), pl.ds(5 * BAND, 7 * BAND)
+
+    def pair_landed(r):
         loads[r].wait()
         arrived(r0.at[r], c_send.at[r], c_recv.at[r], partner)
-        return half[r].astype(F32) + r0[r].astype(F32)
-
-    lo, hi = pl.ds(0, EIGHTH), pl.ds(EIGHTH, EIGHTH)
-    sb[2] = pair_sum(2).astype(BF16)
-    send(sb.at[2, lo], ra, x_send.at[0], x_recv.at[0], xp)
-    send(sb.at[2, hi], rb, x_send.at[1], x_recv.at[1], xm)
-    total = pair_sum(1)
-    s1[...] = total[:EIGHTH]
-    sb[1, hi] = total[EIGHTH:].astype(BF16)
-    send(sb.at[1, hi], rl.at[hi], x_send.at[2], x_recv.at[2], xp)
-    total = pair_sum(3)
-    s3[...] = total[EIGHTH:]
-    sb[3, lo] = total[:EIGHTH].astype(BF16)
-    send(sb.at[3, lo], rr.at[lo], x_send.at[3], x_recv.at[3], xm)
-    qf[...] = pair_sum(0)
-
-    arrived(ra, x_send.at[0], x_recv.at[0], xm)
-    sb[1, lo] = (s1[...] + ra[...].astype(F32)).astype(BF16)
-    send(sb.at[1, lo], rl.at[lo], x_send.at[4], x_recv.at[4], xp)
-    arrived(rb, x_send.at[1], x_recv.at[1], xp)
-    sb[3, hi] = (s3[...] + rb[...].astype(F32)).astype(BF16)
-    send(sb.at[3, hi], rr.at[hi], x_send.at[5], x_recv.at[5], xm)
-
-
-    arrived(rl.at[hi], x_send.at[2], x_recv.at[2], xm)
-    arrived(rr.at[lo], x_send.at[3], x_recv.at[3], xp)
-    arrived(rl.at[lo], x_send.at[4], x_recv.at[4], xm)
-    arrived(rr.at[hi], x_send.at[5], x_recv.at[5], xp)
-    total = qf[...] + rl[...].astype(F32) + rr[...].astype(F32)
-    qf[...] = total
-    qb[...] = total.astype(BF16)
-
-    for d in reversed(NEAR):
-        send(qb.at[rows(up_z(d) * BAND, BAND)], rz.at[d], z_send.at[d], z_recv.at[d],
-             at(up_z(d), x, c))
-
-
-    def from_z(d):
-        return up_z(NZ - d)
+
+    def pair_sum(r, ds):
+        return jnp.concatenate(
+            [half[r, rows(up_z(d) * BAND, BAND), :].astype(F32)
+             + r0[r, rows(up_z(d) * BAND, BAND), :].astype(F32) for d in ds],
+            axis=0,
+        )
+
+    def begin(i, ds, lo, hi):
+        if i == 0:
+            pair_landed(2)
+        total = pair_sum(2, ds).astype(BF16)
+        cut = lo.size
+        sb[2, lo], sb[2, hi] = total[:cut], total[cut:]
+        send(sb.at[2, lo], ra.at[lo], x_send.at[0, i], x_recv.at[0, i], xp)
+        send(sb.at[2, hi], rb.at[hi], x_send.at[1, i], x_recv.at[1, i], xm)
+        if i == 0:
+            pair_landed(1)
+        total = pair_sum(1, ds)
+        s1[lo] = total[:cut]
+        sb[1, hi] = total[cut:].astype(BF16)
+        send(sb.at[1, hi], rl.at[hi], x_send.at[2, i], x_recv.at[2, i], xp)
+        if i == 0:
+            pair_landed(3)
+        total = pair_sum(3, ds)
+        s3[hi] = total[cut:]
+        sb[3, lo] = total[:cut].astype(BF16)
+        send(sb.at[3, lo], rr.at[lo], x_send.at[3, i], x_recv.at[3, i], xm)
+
+    def middle(i, lo, hi):
+        arrived(ra.at[lo], x_send.at[0, i], x_recv.at[0, i], xm)
+        sb[1, lo] = (s1[lo, :] + ra[lo, :].astype(F32)).astype(BF16)
+        send(sb.at[1, lo], rl.at[lo], x_send.at[4, i], x_recv.at[4, i], xp)
+        arrived(rb.at[hi], x_send.at[1, i], x_recv.at[1, i], xp)
+        sb[3, hi] = (s3[hi, :] + rb[hi, :].astype(F32)).astype(BF16)
+        send(sb.at[3, hi], rr.at[hi], x_send.at[5, i], x_recv.at[5, i], xm)
+
+    def finish(i, lo, hi, both, ds):
+        arrived(rl.at[hi], x_send.at[2, i], x_recv.at[2, i], xm)
+        arrived(rr.at[lo], x_send.at[3, i], x_recv.at[3, i], xp)
+        arrived(rl.at[lo], x_send.at[4, i], x_recv.at[4, i], xm)
+        arrived(rr.at[hi], x_send.at[5, i], x_recv.at[5, i], xp)
+        total = qf[both, :] + rl[both, :].astype(F32) + rr[both, :].astype(F32)
+        qf[both] = total
+        qb[both] = total.astype(BF16)
+        for d in ds:
+            send(qb.at[pl.ds((d + 8) % NZ * BAND, BAND)], rz.at[d], z_send.at[d], z_recv.at[d],
+                 at(up_z(d), x, c))
+
+    begin(0, far, far_lo, far_hi)
+    begin(1, near, near_lo, near_hi)
+    pair_landed(0)
+    qf[...] = pair_sum(0, far + near)
+    for d in (3, 9):
+        arrived(p.at[c, x, from_z(d)], pz_send.at[d], pz_recv.at[d], zm)
+    over = 3 - 6 * c
+    band = p.at[c, x, lax.rem(z - over + NZ, NZ)]
+    send(band, band, pz_send.at[6], pz_recv.at[6], at(lax.rem(z + over + NZ, NZ), x, c))
+    for k in (2, 1):
+        band_along(3, k)
+        band_along(9, -k)
+    middle(0, far_lo, far_hi)
+    middle(1, near_lo, near_hi)
+    finish(0, far_lo, far_hi, all_far, (6, 5, 7, 4, 8))
+    finish(1, near_lo, near_hi, all_near, (3, 9, 2, 10, 1, 11))
 
     def bands(r, k=None):
         return p.at[c, up_x(r)] if k is None else p.at[c, up_x(r), pl.ds(k * (NZ // 2), NZ // 2)]
@@ -148,7 +188,7 @@
     def give_bands(r, i):
         send(bands(r), bands(r), pc_send.at[i], pc_recv.at[i], partner)
 
-    for d in NEAR:
+    for d in (1, 11, 2, 10, 4, 8, 5, 7, 6):
         arrived(p.at[c, x, from_z(d)], pz_send.at[d], pz_recv.at[d], zm)
     pass_bands(0, 0, 0, xp)
     pass_bands(0, 1, 1, xm)
@@ -158,7 +198,7 @@
 
     for d in NEAR:
         arrived(rz.at[d], z_send.at[d], z_recv.at[d], zm)
-    total = qf[rows(z * BAND, BAND), :]
+    total = qf[8 * BAND : 9 * BAND, :]
     for d in NEAR:
         total = total + rz[d].astype(F32)
 
@@ -181,9 +221,6 @@
     for d in NEAR:
         arrived(chunk(x, from_z(d)), gz_send.at[d], gz_recv.at[d], zm)
 
-    arrived(bands(2, 0), px_send.at[2, 0], px_recv.at[2, 0], xm)
-    arrived(bands(2, 1), px_send.at[2, 1], px_recv.at[2, 1], xp)
-    give_bands(2, 3)
     def part(r, a, n):
         return g.at[rows((c * NX + up_x(r)) * QUARTER + a, n)]
 
@@ -203,6 +240,22 @@
     send(part(3, 0, QUARTER), part(3, 0, QUARTER), gc_send.at[1, 0], gc_recv.at[1, 0], partner)
     arrived(part(1, 0, EIGHTH), gx_send.at[1, 0], gx_recv.at[1, 0], xp)
     send(part(1, 0, QUARTER), part(1, 0, QUARTER), gc_send.at[2, 0], gc_recv.at[2, 0], partner)
+    arrived(bands(2, 0), px_send.at[2, 0], px_recv.at[2, 0], xm)
+    arrived(bands(2, 1), px_send.at[2, 1], px_recv.at[2, 1], xp)
+    give_bands(2, 3)
+    for i, r in ((0, 0), (1, 3), (2, 1), (3, 2)):
+        arrived(p.at[1 - c, up_x(r)], pc_send.at[i], pc_recv.at[i], partner)
+
+    def place(k, _):
+        d = owner[k]
+        cc, xx, zz = lax.rem(d, NC), lax.rem(d // NC, NX), d // (NC * NX)
+        there = rows(k * BAND, BAND)
+        pls[there, :] = p[cc, xx, zz, 0]
+        prs[there, :] = p[cc, xx, zz, 1]
+        return 0
+
+    lax.fori_loop(0, NZ * NX * NC, place, 0, unroll=8)
+
     arrived(part(2, 0, EIGHTH), gx_send.at[2, 0], gx_recv.at[2, 0], xm)
     arrived(part(2, EIGHTH, EIGHTH), gx_send.at[2, 1], gx_recv.at[2, 1], xp)
     send(part(2, 0, QUARTER), part(2, 0, QUARTER), gc_send.at[3, 0], gc_recv.at[3, 0], partner)
@@ -210,39 +263,39 @@
     for k, r in ((0, 0), (1, 3), (2, 1), (3, 2)):
         theirs = g.at[rows(((1 - c) * NX + up_x(r)) * QUARTER, QUARTER)]
         arrived(theirs, gc_send.at[k, 0], gc_recv.at[k, 0], partner)
-    for i, r in ((0, 0), (1, 3), (2, 1), (3, 2)):
-        arrived(p.at[1 - c, up_x(r)], pc_send.at[i], pc_recv.at[i], partner)
     for made in pending:
         made.wait_send()
 
 
-def gather_all(grad, left, right):
+def gather_all(owner, grad, left, right):
     vmem = pl.BlockSpec(memory_space=pltpu.VMEM)
     dma = pltpu.SemaphoreType.DMA
     return pl.pallas_call(
         exchange,
         out_shape=(
             jax.ShapeDtypeStruct((ROWS, BLK), BF16),
-            jax.ShapeDtypeStruct((NC, NX, NZ, 2, BAND, BLK), BF16),
+            jax.ShapeDtypeStruct((ROWS, BLK), BF16),
+            jax.ShapeDtypeStruct((ROWS, BLK), BF16),
         ),
-        in_specs=[pl.BlockSpec(memory_space=pltpu.HBM)] * 3,
-        out_specs=(vmem, vmem),
+        in_specs=[pl.BlockSpec(memory_space=pltpu.SMEM)] + [pl.BlockSpec(memory_space=pltpu.HBM)] * 3,
+        out_specs=(vmem, vmem, vmem),
         scratch_shapes=[
+            pltpu.VMEM((NC, NX, NZ, 2, BAND, BLK), BF16),
             pltpu.VMEM((NX, QUARTER, BLK), BF16),
             pltpu.VMEM((NX, QUARTER, BLK), BF16),
             pltpu.VMEM((NX, QUARTER, BLK), BF16),
-            pltpu.VMEM((EIGHTH, BLK), BF16),
-            pltpu.VMEM((EIGHTH, BLK), BF16),
+            pltpu.VMEM((QUARTER, BLK), BF16),
+            pltpu.VMEM((QUARTER, BLK), BF16),
             pltpu.VMEM((QUARTER, BLK), BF16),
             pltpu.VMEM((QUARTER, BLK), BF16),
             pltpu.VMEM((QUARTER, BLK), F32),
             pltpu.VMEM((QUARTER, BLK), BF16),
             pltpu.VMEM((NZ, BAND, BLK), BF16),
-            pltpu.VMEM((EIGHTH, BLK), F32),
-            pltpu.VMEM((EIGHTH, BLK), F32),
+            pltpu.VMEM((QUARTER, BLK), F32),
+            pltpu.VMEM((QUARTER, BLK), F32),
             dma((2 + NX,)),
             dma((NX,)), dma((NX,)),
-            dma((6,)), dma((6,)),
+            dma((6, 2)), dma((6, 2)),
             dma((NZ,)), dma((NZ,)),
             dma((NZ,)), dma((NZ,)),
             dma((3, NZ)), dma((3, NZ)),
@@ -254,21 +307,16 @@
         compiler_params=pltpu.CompilerParams(
             collective_id=0, has_side_effects=True, vmem_limit_bytes=40 << 20
         ),
-    )(grad, left, right)
-
-
-def dots(owner, g, p, left_factor, right_factor, direction, left_out, right_out, pls, prs):
+    )(owner, grad, left, right)
+
+
+def dots(owner, g, pls, prs, left_factor, right_factor, direction, left_out, right_out):
     me = lax.axis_index("dp")
 
-    def place(k, own):
-        d = owner[k]
-        cc, xx, zz = lax.rem(d, NC), lax.rem(d // NC, NX), d // (NC * NX)
-        at = pl.ds(pl.multiple_of(k * BAND, BAND), BAND)
-        pls[at, :] = p[cc, xx, zz, 0]
-        prs[at, :] = p[cc, xx, zz, 1]
-        return jnp.where(d == me, k, own)
-
-    own = lax.fori_loop(0, NZ * NX * NC, place, jnp.int32(0), unroll=8)
+    def find(k, own):
+        return jnp.where(owner[k] == me, k, own)
+
+    own = lax.fori_loop(0, NZ * NX * NC, find, jnp.int32(0), unroll=8)
     start = own * BAND
     block = start // BLK
     within = start - block * BLK
@@ -289,7 +337,7 @@
         direction[at, :] = jnp.dot(pls[at, :], mixed, preferred_element_type=F32).astype(BF16)
 
 
-def precondition(owner, g, p, left_factor, right_factor):
+def precondition(owner, g, pls, prs, left_factor, right_factor):
     vmem = pl.BlockSpec(memory_space=pltpu.VMEM)
     return pl.pallas_call(
         dots,
@@ -298,16 +346,16 @@
             jax.ShapeDtypeStruct((BAND, BLK), F32),
             jax.ShapeDtypeStruct((BAND, BLK), F32),
         ),
-        in_specs=[pl.BlockSpec(memory_space=pltpu.SMEM)] + [vmem] * 4,
+        in_specs=[pl.BlockSpec(memory_space=pltpu.SMEM)] + [vmem] * 5,
         out_specs=(vmem, vmem, vmem),
-        scratch_shapes=[pltpu.VMEM((ROWS, BLK), BF16), pltpu.VMEM((ROWS, BLK), BF16)],
         compiler_params=pltpu.CompilerParams(vmem_limit_bytes=40 << 20),
-    )(owner, g, p, left_factor, right_factor)
+    )(owner, g, pls, prs, left_factor, right_factor)
 
 
 def shards(partial_grads, band_owner, left_factor, right_factor, left_root, right_root):
-    g, p = gather_all(partial_grads, left_root, right_root)
-    return precondition(band_owner, g, p, left_factor, right_factor)
+    held = [pltpu.with_memory_space_constraint(v, pltpu.HBM) for v in (band_owner, partial_grads, left_root, right_root)]
+    g, pls, prs = gather_all(*held)
+    return precondition(band_owner, g, pls, prs, left_factor, right_factor)
 
 
 def solution(mesh):

time: 68.9 us -> 63.5 us (0.922)
  local copies, waits for them, and re-layouts: 2.85 us -> 0.01 us
  Pallas kernels: 65 us -> 62.6 us
    unnamed x12 -> x6, local copies, waits for them, and re-layouts: 2.85 us -> 0.01 us
    pallas_call x1, Pallas kernels: 5.55 us -> 4.31 us  [precondition(): pl.pallas_call(dots, out_shape=(jax.ShapeDtypeStruct((ROWS, BLK), BF16),...]
    pallas_call x1, Pallas kernels: 59.5 us -> 58.3 us  [gather_all(): pl.pallas_call(exchange, out_shape=(jax.ShapeDtypeStruct((ROWS, BLK), BF1...]
where the time goes in v3:
time: 63.5 us; the launch traced here: 63.3 us
  Pallas kernels  62.6 us (99%)
  between operations  0.69 us (1%)
    pallas_call x1, Pallas kernels, gather_all(): pl.pallas_call(exchange, out_shape=(jax.ShapeDtypeStruct((ROWS, BLK), BF1...  58.3 us
    pallas_call x1, Pallas kernels, precondition(): pl.pallas_call(dots, out_shape=(jax.ShapeDtypeStruct((ROWS, BLK), BF16),...  4.31 us

profile of v3, /device:TPU:1, one launch (start us, length us, event | category | flops | bytes accessed | tf_op | source)
XLA Modules:
  0.0 63.3 jit_solution(899354766152853164)
XLA Ops:
  0.6 0.0 copy-start.2
  0.6 0.0 copy-start.1
  0.7 0.0 copy-start
  0.7 58.3 %shard_map.85 = (bf16[1536,512]{1,0:T(8,128)(2,1)S(1)}, bf16[1536,512]{1,0:T(8,128)(2,1)S(1)}, bf16[1536,512]{1,0:T(8,128)(2,1)S(1)}) custom-call(s32[96]{0:T(128)} %owner.3, bf16[1,1536,512]{2,1,0:T(8,128)(2,1)} %grad.1, bf16[16,512]{1,0:T(8,128)(2,1)} %left.1, bf16[16,512]{1,0:T(8,128)(2,1)} %right.1), custom_call_target="tpu_custom_call" | custom-call | tf_op jit(solution)/shard_map/pallas_call | solution.py:273
  58.9 0.0 copy-done.2
  58.9 0.0 copy-done.1
  59.0 0.0 copy-done
  59.0 4.3 %shard_map.86 = (bf16[1536,512]{1,0:T(8,128)(2,1)}, f32[16,512]{1,0:T(8,128)}, f32[16,512]{1,0:T(8,128)}) custom-call(s32[96]{0:T(128)S(1)} %copy-done.2, bf16[1536,512]{1,0:T(8,128)(2,1)S(1)} %get-tuple-element.6.g, bf16[1536,512]{1,0:T(8,128)(2,1)S(1)} %get-tuple-element.7.pls, bf16[1536,512]{1,0:T(8,128)(2,1)S(1)} %get-tuple-element.8.prs, ...), custom_call_target="tpu_custom_call" | custom-call | tf_op jit(solution)/shard_map/pallas_call | solution.py:342
Async XLA Ops:
  0.6 58.3 %copy-start.2 = (s32[96]{0:T(128)S(1)}, s32[96]{0:T(128)}, u32[]{:S(2)}) copy-start(s32[96]{0:T(128)} %owner.3) | copy-start | bytes 1156
  0.6 58.3 %copy-start.1 = (f32[16,512]{1,0:T(8,128)S(1)}, f32[16,512]{1,0:T(8,128)}, u32[]{:S(2)}) copy-start(f32[16,512]{1,0:T(8,128)} %right_factor.1) | copy-start | bytes 98308
  0.7 58.3 %copy-start = (f32[16,512]{1,0:T(8,128)S(1)}, f32[16,512]{1,0:T(8,128)}, u32[]{:S(2)}) copy-start(f32[16,512]{1,0:T(8,128)} %left_factor.1) | copy-start | bytes 98308

commit v4 on v3

--- a/solution.py
+++ b/solution.py
@@ -26,7 +26,7 @@
     owner, grad, left, right, g, pls, prs,
     p, half, r0, sb, ra, rb, rl, rr, qf, qb, rz, s1, s3,
     sem_local, c_send, c_recv, x_send, x_recv, z_send, z_recv,
-    gz_send, gz_recv, gx_send, gx_recv, gc_send, gc_recv,
+    gz_send, gz_recv, gx_send, gx_recv, gy_send, gy_recv, gc_send, gc_recv, go_send, go_recv,
     px_send, px_recv, pz_send, pz_recv, pc_send, pc_recv,
 ):
     me = lax.axis_index("dp")
@@ -78,7 +78,7 @@
     ]
     loads = {
         r: pltpu.make_async_copy(
-            grad.at[0, rows(c * HALF + up_x(r) * QUARTER, QUARTER)], half.at[r], sem_local.at[2 + r]
+            grad.at[c, :, up_x(r)], half.at[r], sem_local.at[2 + r]
         )
         for r in (2, 1, 3, 0)
     }
@@ -88,7 +88,7 @@
 
     for r in (2, 1, 3, 0):
         send(
-            grad.at[0, rows((1 - c) * HALF + up_x(r) * QUARTER, QUARTER)],
+            grad.at[1 - c, :, up_x(r)],
             r0.at[r], c_send.at[r], c_recv.at[r], partner,
         )
     for one in own:
@@ -116,8 +116,7 @@
 
     def pair_sum(r, ds):
         return jnp.concatenate(
-            [half[r, rows(up_z(d) * BAND, BAND), :].astype(F32)
-             + r0[r, rows(up_z(d) * BAND, BAND), :].astype(F32) for d in ds],
+            [half[r, up_z(d)].astype(F32) + r0[r, up_z(d)].astype(F32) for d in ds],
             axis=0,
         )
 
@@ -202,67 +201,132 @@
     for d in NEAR:
         total = total + rz[d].astype(F32)
 
-    def chunk(xx, zz):
-        return g.at[rows((c * NX * NZ + xx * NZ + zz) * BAND, BAND)]
-
-    g[rows((c * NX * NZ + x * NZ + z) * BAND, BAND), :] = total.astype(BF16)
-
-    own_chunk = chunk(x, z)
-    for d in reversed(NEAR):
-        send(own_chunk, own_chunk, gz_send.at[d], gz_recv.at[d], at(up_z(d), x, c))
-    arrived(bands(3, 0), px_send.at[0, 0], px_recv.at[0, 0], xm)
-    pass_bands(3, 0, 2, xp)
-    arrived(bands(1, 1), px_send.at[1, 1], px_recv.at[1, 1], xp)
-    pass_bands(1, 1, 2, xm)
-    arrived(bands(3, 1), px_send.at[0, 1], px_recv.at[0, 1], xm)
-    give_bands(3, 1)
-    arrived(bands(1, 0), px_send.at[1, 0], px_recv.at[1, 0], xp)
-    give_bands(1, 2)
-    for d in NEAR:
-        arrived(chunk(x, from_z(d)), gz_send.at[d], gz_recv.at[d], zm)
-
-    def part(r, a, n):
-        return g.at[rows((c * NX + up_x(r)) * QUARTER + a, n)]
-
-    mine = part(0, 0, QUARTER)
-    lo_half, hi_half = part(0, 0, EIGHTH), part(0, EIGHTH, EIGHTH)
-    send(lo_half, lo_half, gx_send.at[0, 0], gx_recv.at[0, 0], xp)
-    send(hi_half, hi_half, gx_send.at[1, 1], gx_recv.at[1, 1], xm)
-    send(hi_half, hi_half, gx_send.at[0, 1], gx_recv.at[0, 1], xp)
-    send(lo_half, lo_half, gx_send.at[1, 0], gx_recv.at[1, 0], xm)
-    send(mine, mine, gc_send.at[0, 0], gc_recv.at[0, 0], partner)
-    below, above = part(3, 0, EIGHTH), part(1, EIGHTH, EIGHTH)
-    arrived(below, gx_send.at[0, 0], gx_recv.at[0, 0], xm)
-    send(below, below, gx_send.at[2, 0], gx_recv.at[2, 0], xp)
-    arrived(above, gx_send.at[1, 1], gx_recv.at[1, 1], xp)
-    send(above, above, gx_send.at[2, 1], gx_recv.at[2, 1], xm)
-    arrived(part(3, EIGHTH, EIGHTH), gx_send.at[0, 1], gx_recv.at[0, 1], xm)
-    send(part(3, 0, QUARTER), part(3, 0, QUARTER), gc_send.at[1, 0], gc_recv.at[1, 0], partner)
-    arrived(part(1, 0, EIGHTH), gx_send.at[1, 0], gx_recv.at[1, 0], xp)
-    send(part(1, 0, QUARTER), part(1, 0, QUARTER), gc_send.at[2, 0], gc_recv.at[2, 0], partner)
-    arrived(bands(2, 0), px_send.at[2, 0], px_recv.at[2, 0], xm)
-    arrived(bands(2, 1), px_send.at[2, 1], px_recv.at[2, 1], xp)
-    give_bands(2, 3)
-    for i, r in ((0, 0), (1, 3), (2, 1), (3, 2)):
-        arrived(p.at[1 - c, up_x(r)], pc_send.at[i], pc_recv.at[i], partner)
-
-    def place(k, _):
-        d = owner[k]
-        cc, xx, zz = lax.rem(d, NC), lax.rem(d // NC, NX), d // (NC * NX)
-        there = rows(k * BAND, BAND)
-        pls[there, :] = p[cc, xx, zz, 0]
-        prs[there, :] = p[cc, xx, zz, 1]
-        return 0
-
-    lax.fori_loop(0, NZ * NX * NC, place, 0, unroll=8)
-
-    arrived(part(2, 0, EIGHTH), gx_send.at[2, 0], gx_recv.at[2, 0], xm)
-    arrived(part(2, EIGHTH, EIGHTH), gx_send.at[2, 1], gx_recv.at[2, 1], xp)
-    send(part(2, 0, QUARTER), part(2, 0, QUARTER), gc_send.at[3, 0], gc_recv.at[3, 0], partner)
-
-    for k, r in ((0, 0), (1, 3), (2, 1), (3, 2)):
-        theirs = g.at[rows(((1 - c) * NX + up_x(r)) * QUARTER, QUARTER)]
-        arrived(theirs, gc_send.at[k, 0], gc_recv.at[k, 0], partner)
+    g[c, z, x] = total.astype(BF16)
+    own_chunk = g.at[c, z, x]
+
+    def bands_near():
+        arrived(bands(3, 0), px_send.at[0, 0], px_recv.at[0, 0], xm)
+        pass_bands(3, 0, 2, xp)
+        arrived(bands(1, 1), px_send.at[1, 1], px_recv.at[1, 1], xp)
+        pass_bands(1, 1, 2, xm)
+        arrived(bands(3, 1), px_send.at[0, 1], px_recv.at[0, 1], xm)
+        give_bands(3, 1)
+        arrived(bands(1, 0), px_send.at[1, 0], px_recv.at[1, 0], xp)
+        give_bands(1, 2)
+
+    def bands_far():
+        arrived(bands(2, 0), px_send.at[2, 0], px_recv.at[2, 0], xm)
+        arrived(bands(2, 1), px_send.at[2, 1], px_recv.at[2, 1], xp)
+        give_bands(2, 3)
+        for i, r in ((0, 0), (1, 3), (2, 1), (3, 2)):
+            arrived(p.at[1 - c, up_x(r)], pc_send.at[i], pc_recv.at[i], partner)
+
+        def place(k, _):
+            d = owner[k]
+            cc, xx, zz = lax.rem(d, NC), lax.rem(d // NC, NX), d // (NC * NX)
+            there = rows(k * BAND, BAND)
+            pls[there, :] = p[cc, xx, zz, 0]
+            prs[there, :] = p[cc, xx, zz, 1]
+            return 0
+
+        lax.fori_loop(0, NZ * NX * NC, place, 0, unroll=8)
+
+    def z_then_x():
+        def part(r, k=None):
+            return g.at[c, :, up_x(r)] if k is None else g.at[c, pl.ds(k * (NZ // 2), NZ // 2), up_x(r)]
+
+        def on(r, k, i, dev):
+            send(part(r, k), part(r, k), gx_send.at[i, k], gx_recv.at[i, k], dev)
+
+        def got(r, k, i):
+            arrived(part(r, k), gx_send.at[i, k], gx_recv.at[i, k], xp)
+
+        def give(r, i):
+            send(part(r), part(r), gc_send.at[i], gc_recv.at[i], partner)
+
+        for d in reversed(NEAR):
+            send(own_chunk, own_chunk, gz_send.at[d], gz_recv.at[d], at(up_z(d), x, c))
+        bands_near()
+        for d in NEAR:
+            arrived(g.at[c, from_z(d), x], gz_send.at[d], gz_recv.at[d], zm)
+        on(0, 0, 0, xp)
+        on(0, 1, 1, xm)
+        on(0, 1, 0, xp)
+        on(0, 0, 1, xm)
+        give(0, 0)
+        got(3, 0, 0)
+        on(3, 0, 2, xp)
+        got(1, 1, 1)
+        on(1, 1, 2, xm)
+        got(3, 1, 0)
+        give(3, 1)
+        got(1, 0, 1)
+        give(1, 2)
+        bands_far()
+        got(2, 0, 2)
+        got(2, 1, 2)
+        give(2, 3)
+        for d in [0] + NEAR:
+            arrived(g.at[1 - c, from_z(d)], go_send.at[d], go_recv.at[d], partner)
+
+    def x_then_z():
+        def row(d):
+            return g.at[c, from_z(d)]
+
+        def on(d, k):
+            to = (d + k) % NZ
+            send(row(d), row(d), gz_send.at[to], gz_recv.at[to], at(up_z(k % NZ), x, c))
+
+        def got(*ds):
+            for d in ds:
+                arrived(row(d), gz_send.at[d], gz_recv.at[d], zm)
+
+        def give(*ds):
+            for d in ds:
+                send(row(d), row(d), go_send.at[d], go_recv.at[d], partner)
+
+        for k in (2, 1, 3):
+            send(own_chunk, own_chunk, gy_send.at[k], gy_recv.at[k], at(z, up_x(k), c))
+        for k in (1, 3, 2):
+            arrived(g.at[c, z, up_x(NX - k)], gy_send.at[k], gy_recv.at[k], xp)
+        for k in (3, -3, 2, -2, 1, -1):
+            on(0, k)
+        give(0)
+        bands_near()
+        got(3, 9)
+        six = g.at[c, up_z(3)]
+        send(six, six, gz_send.at[6], gz_recv.at[6], at(up_z(NZ - 3), x, c))
+        for k in (2, 1):
+            on(3, k)
+            on(9, -k)
+        give(3, 9)
+        got(1, 11, 2, 10)
+        give(1, 11, 2, 10)
+        bands_far()
+        for d in (4, 8, 5, 7, 6):
+            got(d)
+            give(d)
+        for i, r in ((0, 0), (1, 3), (2, 1), (3, 2)):
+            arrived(g.at[1 - c, :, up_x(r)], gc_send.at[i], gc_recv.at[i], partner)
+
+    started = list(pending)
+    pending.clear()
+
+    def finish_with(part):
+        part()
+        for made in pending:
+            made.wait_send()
+        pending.clear()
+
+    @pl.when(c == 0)
+    def _():
+        finish_with(z_then_x)
+
+    @pl.when(c == 1)
+    def _():
+        finish_with(x_then_z)
+
+    pending.extend(started)
     for made in pending:
         made.wait_send()
 
@@ -273,7 +337,7 @@
     return pl.pallas_call(
         exchange,
         out_shape=(
-            jax.ShapeDtypeStruct((ROWS, BLK), BF16),
+            jax.ShapeDtypeStruct((NC, NZ, NX, BAND, BLK), BF16),
             jax.ShapeDtypeStruct((ROWS, BLK), BF16),
             jax.ShapeDtypeStruct((ROWS, BLK), BF16),
         ),
@@ -281,8 +345,8 @@
         out_specs=(vmem, vmem, vmem),
         scratch_shapes=[
             pltpu.VMEM((NC, NX, NZ, 2, BAND, BLK), BF16),
-            pltpu.VMEM((NX, QUARTER, BLK), BF16),
-            pltpu.VMEM((NX, QUARTER, BLK), BF16),
+            pltpu.VMEM((NX, NZ, BAND, BLK), BF16),
+            pltpu.VMEM((NX, NZ, BAND, BLK), BF16),
             pltpu.VMEM((NX, QUARTER, BLK), BF16),
             pltpu.VMEM((QUARTER, BLK), BF16),
             pltpu.VMEM((QUARTER, BLK), BF16),
@@ -298,8 +362,10 @@
             dma((6, 2)), dma((6, 2)),
             dma((NZ,)), dma((NZ,)),
             dma((NZ,)), dma((NZ,)),
-            dma((3, NZ)), dma((3, NZ)),
-            dma((NX, NZ)), dma((NX, NZ)),
+            dma((3, 2)), dma((3, 2)),
+            dma((NX,)), dma((NX,)),
+            dma((NX,)), dma((NX,)),
+            dma((NZ,)), dma((NZ,)),
             dma((3, 2)), dma((3, 2)),
             dma((NZ,)), dma((NZ,)),
             dma((NX,)), dma((NX,)),
@@ -353,9 +419,10 @@
 
 
 def shards(partial_grads, band_owner, left_factor, right_factor, left_root, right_root):
-    held = [pltpu.with_memory_space_constraint(v, pltpu.HBM) for v in (band_owner, partial_grads, left_root, right_root)]
+    grad = partial_grads.reshape(NC, NZ, NX, BAND, BLK)
+    held = [pltpu.with_memory_space_constraint(v, pltpu.HBM) for v in (band_owner, grad, left_root, right_root)]
     g, pls, prs = gather_all(*held)
-    return precondition(band_owner, g, pls, prs, left_factor, right_factor)
+    return precondition(band_owner, g.reshape(ROWS, BLK), pls, prs, left_factor, right_factor)
 
 
 def solution(mesh):

time: 63.5 us -> 60.3 us (0.950)
  Pallas kernels: 62.6 us -> 59.4 us
    pallas_call x1, Pallas kernels: 58.3 us -> 55.1 us  [gather_all(): pl.pallas_call(exchange, out_shape=(jax.ShapeDtypeStruct((NC, NZ, NX, BAN...]
where the time goes in v4:
time: 60.3 us; the launch traced here: 60.1 us
  Pallas kernels  59.4 us (99%)
  between operations  0.69 us (1%)
    pallas_call x1, Pallas kernels, gather_all(): pl.pallas_call(exchange, out_shape=(jax.ShapeDtypeStruct((NC, NZ, NX, BAN...  55.1 us
    pallas_call x1, Pallas kernels, precondition(): pl.pallas_call(dots, out_shape=(jax.ShapeDtypeStruct((ROWS, BLK), BF16),...  4.31 us

profile of v4, /device:TPU:1, one launch (start us, length us, event | category | flops | bytes accessed | tf_op | source)
XLA Modules:
  0.0 60.1 jit_solution(15372713812400339325)
XLA Ops:
  0.6 0.0 copy-start.2
  0.6 0.0 copy-start.1
  0.7 0.0 copy-start
  0.7 55.1 %shard_map.85 = (bf16[2,12,4,16,512]{4,3,2,1,0:T(8,128)(2,1)S(1)}, bf16[1536,512]{1,0:T(8,128)(2,1)S(1)}, bf16[1536,512]{1,0:T(8,128)(2,1)S(1)}) custom-call(s32[96]{0:T(128)} %owner.3, bf16[2,12,4,16,512]{4,3,2,1,0:T(8,128)(2,1)} %bitcast.3, bf16[16,512]{1,0:T(8,128)(2,1)} %left.1, bf16[16,512]{1,0:T(8,128)(2,1)} %right.1), custom_call_target="tpu_custom_call" | custom-call | tf_op jit(solution)/shard_map/pallas_call | solution.py:337
  55.8 0.0 copy-done.2
  55.8 0.0 copy-done.1
  55.8 0.0 copy-done
  55.8 4.3 %shard_map.86 = (bf16[1536,512]{1,0:T(8,128)(2,1)}, f32[16,512]{1,0:T(8,128)}, f32[16,512]{1,0:T(8,128)}) custom-call(s32[96]{0:T(128)S(1)} %copy-done.2, bf16[1536,512]{1,0:T(8,128)(2,1)S(1)} %bitcast.2, bf16[1536,512]{1,0:T(8,128)(2,1)S(1)} %get-tuple-element.7.pls, bf16[1536,512]{1,0:T(8,128)(2,1)S(1)} %get-tuple-element.8.prs, f32[16,512]{1,0:T(8,128)S(1)} %copy-done, ...), custom_call_target="tpu_custom_call" | custom-call | tf_op jit(solution)/shard_map/pallas_call | solution.py:408
Async XLA Ops:
  0.6 55.1 %copy-start.2 = (s32[96]{0:T(128)S(1)}, s32[96]{0:T(128)}, u32[]{:S(2)}) copy-start(s32[96]{0:T(128)} %owner.3) | copy-start | bytes 1156
  0.6 55.1 %copy-start.1 = (f32[16,512]{1,0:T(8,128)S(1)}, f32[16,512]{1,0:T(8,128)}, u32[]{:S(2)}) copy-start(f32[16,512]{1,0:T(8,128)} %right_factor.1) | copy-start | bytes 98308
  0.7 55.1 %copy-start = (f32[16,512]{1,0:T(8,128)S(1)}, f32[16,512]{1,0:T(8,128)}, u32[]{:S(2)}) copy-start(f32[16,512]{1,0:T(8,128)} %left_factor.1) | copy-start | bytes 98308

commit v5 on v4

--- a/solution.py
+++ b/solution.py
@@ -26,7 +26,7 @@
     owner, grad, left, right, g, pls, prs,
     p, half, r0, sb, ra, rb, rl, rr, qf, qb, rz, s1, s3,
     sem_local, c_send, c_recv, x_send, x_recv, z_send, z_recv,
-    gz_send, gz_recv, gx_send, gx_recv, gy_send, gy_recv, gc_send, gc_recv, go_send, go_recv,
+    gz_send, gz_recv, gy_send, gy_recv, gc_send, gc_recv, go_send, go_recv,
     px_send, px_recv, pz_send, pz_recv, pc_send, pc_recv,
 ):
     me = lax.axis_index("dp")
@@ -63,8 +63,8 @@
         copy(dst, dst, ss, rs, dev).wait_recv()
 
     barrier = pltpu.get_barrier_semaphore()
-    others = [partner] + [at(z, up_x(k), c) for k in (1, 2, 3)]
-    others += [at(up_z(k), x, c) for k in NEAR]
+    others = [at(up_z(k), x, c) for k in reversed(NEAR)]
+    others += [at(z, up_x(k), c) for k in (2, 1, 3)] + [partner]
     for dev in others:
         pl.semaphore_signal(barrier, inc=1, device_id={"dp": dev}, device_id_type=MESH)
 
@@ -218,6 +218,8 @@
         arrived(bands(2, 0), px_send.at[2, 0], px_recv.at[2, 0], xm)
         arrived(bands(2, 1), px_send.at[2, 1], px_recv.at[2, 1], xp)
         give_bands(2, 3)
+
+    def bands_in_order():
         for i, r in ((0, 0), (1, 3), (2, 1), (3, 2)):
             arrived(p.at[1 - c, up_x(r)], pc_send.at[i], pc_recv.at[i], partner)
 
@@ -235,12 +237,6 @@
         def part(r, k=None):
             return g.at[c, :, up_x(r)] if k is None else g.at[c, pl.ds(k * (NZ // 2), NZ // 2), up_x(r)]
 
-        def on(r, k, i, dev):
-            send(part(r, k), part(r, k), gx_send.at[i, k], gx_recv.at[i, k], dev)
-
-        def got(r, k, i):
-            arrived(part(r, k), gx_send.at[i, k], gx_recv.at[i, k], xp)
-
         def give(r, i):
             send(part(r), part(r), gc_send.at[i], gc_recv.at[i], partner)
 
@@ -249,23 +245,14 @@
         bands_near()
         for d in NEAR:
             arrived(g.at[c, from_z(d), x], gz_send.at[d], gz_recv.at[d], zm)
-        on(0, 0, 0, xp)
-        on(0, 1, 1, xm)
-        on(0, 1, 0, xp)
-        on(0, 0, 1, xm)
+        for k in (2, 1, 3):
+            send(part(0), part(0), gy_send.at[k], gy_recv.at[k], at(z, up_x(k), c))
         give(0, 0)
-        got(3, 0, 0)
-        on(3, 0, 2, xp)
-        got(1, 1, 1)
-        on(1, 1, 2, xm)
-        got(3, 1, 0)
-        give(3, 1)
-        got(1, 0, 1)
-        give(1, 2)
         bands_far()
-        got(2, 0, 2)
-        got(2, 1, 2)
-        give(2, 3)
+        for k, i in ((1, 1), (3, 2), (2, 3)):
+            arrived(part(NX - k), gy_send.at[k], gy_recv.at[k], xp)
+            give(NX - k, i)
+        bands_in_order()
         for d in [0] + NEAR:
             arrived(g.at[1 - c, from_z(d)], go_send.at[d], go_recv.at[d], partner)
 
@@ -306,6 +293,7 @@
         for d in (4, 8, 5, 7, 6):
             got(d)
             give(d)
+        bands_in_order()
         for i, r in ((0, 0), (1, 3), (2, 1), (3, 2)):
             arrived(g.at[1 - c, :, up_x(r)], gc_send.at[i], gc_recv.at[i], partner)
 
@@ -362,7 +350,6 @@
             dma((6, 2)), dma((6, 2)),
             dma((NZ,)), dma((NZ,)),
             dma((NZ,)), dma((NZ,)),
-            dma((3, 2)), dma((3, 2)),
             dma((NX,)), dma((NX,)),
             dma((NX,)), dma((NX,)),
             dma((NZ,)), dma((NZ,)),

time: 60.3 us -> 59.8 us (level)
  no operation moved by 1% of the time
where the time goes in v5:
time: 59.8 us; the launch traced here: 59.6 us
  Pallas kernels  58.9 us (98%)
  between operations  0.69 us (1%)
    pallas_call x1, Pallas kernels, gather_all(): pl.pallas_call(exchange, out_shape=(jax.ShapeDtypeStruct((NC, NZ, NX, BAN...  54.6 us
    pallas_call x1, Pallas kernels, precondition(): pl.pallas_call(dots, out_shape=(jax.ShapeDtypeStruct((ROWS, BLK), BF16),...  4.31 us

profile of v5, /device:TPU:1, one launch (start us, length us, event | category | flops | bytes accessed | tf_op | source)
XLA Modules:
  0.0 59.6 jit_solution(12924514504992752890)
XLA Ops:
  0.6 0.0 copy-start.2
  0.6 0.0 copy-start.1
  0.7 0.0 copy-start
  0.7 54.6 %shard_map.85 = (bf16[2,12,4,16,512]{4,3,2,1,0:T(8,128)(2,1)S(1)}, bf16[1536,512]{1,0:T(8,128)(2,1)S(1)}, bf16[1536,512]{1,0:T(8,128)(2,1)S(1)}) custom-call(s32[96]{0:T(128)} %owner.3, bf16[2,12,4,16,512]{4,3,2,1,0:T(8,128)(2,1)} %bitcast.3, bf16[16,512]{1,0:T(8,128)(2,1)} %left.1, bf16[16,512]{1,0:T(8,128)(2,1)} %right.1), custom_call_target="tpu_custom_call" | custom-call | tf_op jit(solution)/shard_map/pallas_call | solution.py:325
  55.3 0.0 copy-done.2
  55.3 0.0 copy-done.1
  55.3 0.0 copy-done
  55.3 4.3 %shard_map.86 = (bf16[1536,512]{1,0:T(8,128)(2,1)}, f32[16,512]{1,0:T(8,128)}, f32[16,512]{1,0:T(8,128)}) custom-call(s32[96]{0:T(128)S(1)} %copy-done.2, bf16[1536,512]{1,0:T(8,128)(2,1)S(1)} %bitcast.2, bf16[1536,512]{1,0:T(8,128)(2,1)S(1)} %get-tuple-element.7.pls, bf16[1536,512]{1,0:T(8,128)(2,1)S(1)} %get-tuple-element.8.prs, f32[16,512]{1,0:T(8,128)S(1)} %copy-done, ...), custom_call_target="tpu_custom_call" | custom-call | tf_op jit(solution)/shard_map/pallas_call | solution.py:395
Async XLA Ops:
  0.6 54.6 %copy-start.2 = (s32[96]{0:T(128)S(1)}, s32[96]{0:T(128)}, u32[]{:S(2)}) copy-start(s32[96]{0:T(128)} %owner.3) | copy-start | bytes 1156
  0.6 54.6 %copy-start.1 = (f32[16,512]{1,0:T(8,128)S(1)}, f32[16,512]{1,0:T(8,128)}, u32[]{:S(2)}) copy-start(f32[16,512]{1,0:T(8,128)} %right_factor.1) | copy-start | bytes 98308
  0.7 54.6 %copy-start = (f32[16,512]{1,0:T(8,128)S(1)}, f32[16,512]{1,0:T(8,128)}, u32[]{:S(2)}) copy-start(f32[16,512]{1,0:T(8,128)} %left_factor.1) | copy-start | bytes 98308

commit v6 on v5

--- a/solution.py
+++ b/solution.py
@@ -243,14 +243,33 @@
         for d in reversed(NEAR):
             send(own_chunk, own_chunk, gz_send.at[d], gz_recv.at[d], at(up_z(d), x, c))
         bands_near()
-        for d in NEAR:
-            arrived(g.at[c, from_z(d), x], gz_send.at[d], gz_recv.at[d], zm)
-        for k in (2, 1, 3):
-            send(part(0), part(0), gy_send.at[k], gy_recv.at[k], at(z, up_x(k), c))
+        six = NZ // 2
+        base = z // six * six
+        other = six - base
+
+        def half_of(r, start):
+            return g.at[c, pl.ds(start, six), up_x(r)]
+
+        def got_z(zz):
+            d = lax.rem(z - zz + NZ, NZ)
+            arrived(g.at[c, zz, x], gz_send.at[d], gz_recv.at[d], zm)
+
+        def on(h, start):
+            for k in (2, 1, 3):
+                send(half_of(0, start), half_of(0, start),
+                     gy_send.at[h, k], gy_recv.at[h, k], at(z, up_x(k), c))
+
+        for k in (1, 5, 2, 4, 3):
+            got_z(base + lax.rem(z - base + k, six))
+        on(0, base)
+        for k in range(six):
+            got_z(other + k)
+        on(1, other)
         give(0, 0)
         bands_far()
         for k, i in ((1, 1), (3, 2), (2, 3)):
-            arrived(part(NX - k), gy_send.at[k], gy_recv.at[k], xp)
+            arrived(half_of(NX - k, base), gy_send.at[0, k], gy_recv.at[0, k], xp)
+            arrived(half_of(NX - k, other), gy_send.at[1, k], gy_recv.at[1, k], xp)
             give(NX - k, i)
         bands_in_order()
         for d in [0] + NEAR:
@@ -273,9 +292,9 @@
                 send(row(d), row(d), go_send.at[d], go_recv.at[d], partner)
 
         for k in (2, 1, 3):
-            send(own_chunk, own_chunk, gy_send.at[k], gy_recv.at[k], at(z, up_x(k), c))
+            send(own_chunk, own_chunk, gy_send.at[0, k], gy_recv.at[0, k], at(z, up_x(k), c))
         for k in (1, 3, 2):
-            arrived(g.at[c, z, up_x(NX - k)], gy_send.at[k], gy_recv.at[k], xp)
+            arrived(g.at[c, z, up_x(NX - k)], gy_send.at[0, k], gy_recv.at[0, k], xp)
         for k in (3, -3, 2, -2, 1, -1):
             on(0, k)
         give(0)
@@ -350,7 +369,7 @@
             dma((6, 2)), dma((6, 2)),
             dma((NZ,)), dma((NZ,)),
             dma((NZ,)), dma((NZ,)),
-            dma((NX,)), dma((NX,)),
+            dma((2, NX)), dma((2, NX)),
             dma((NX,)), dma((NX,)),
             dma((NZ,)), dma((NZ,)),
             dma((3, 2)), dma((3, 2)),
@@ -384,10 +403,20 @@
     column = lax.dot_general(onehot, gb, last, preferred_element_type=F32).astype(BF16)
     right_term = jnp.dot(column, gb, preferred_element_type=F32)
     right_out[...] = BETA * right_factor[...] + (1.0 - BETA) * right_term
-    for b in range(NB):
+    def mix(b):
         at = pl.ds(b * BLK, BLK)
-        mixed = jnp.dot(g[at, :], prs[at, :], preferred_element_type=F32).astype(BF16)
+        return jnp.dot(g[at, :], prs[at, :], preferred_element_type=F32).astype(BF16)
+
+    def direct(b, mixed):
+        at = pl.ds(b * BLK, BLK)
         direction[at, :] = jnp.dot(pls[at, :], mixed, preferred_element_type=F32).astype(BF16)
+
+    mixed = mix(0)
+    for b in range(1, NB):
+        later = mix(b)
+        direct(b - 1, mixed)
+        mixed = later
+    direct(NB - 1, mixed)
 
 
 def precondition(owner, g, pls, prs, left_factor, right_factor):

time: 59.8 us -> 59.7 us (level)
  no operation moved by 1% of the time
where the time goes in v6:
time: 59.7 us; the launch traced here: 59.5 us
  Pallas kernels  58.8 us (98%)
  between operations  0.69 us (1%)
    pallas_call x1, Pallas kernels, gather_all(): pl.pallas_call(exchange, out_shape=(jax.ShapeDtypeStruct((NC, NZ, NX, BAN...  54.7 us
    pallas_call x1, Pallas kernels, precondition(): pl.pallas_call(dots, out_shape=(jax.ShapeDtypeStruct((ROWS, BLK), BF16),...  4.12 us

profile of v6, /device:TPU:1, one launch (start us, length us, event | category | flops | bytes accessed | tf_op | source)
XLA Modules:
  0.0 59.5 jit_solution(790722356525271584)
XLA Ops:
  0.6 0.0 copy-start.2
  0.6 0.0 copy-start.1
  0.7 0.0 copy-start
  0.7 54.7 %shard_map.85 = (bf16[2,12,4,16,512]{4,3,2,1,0:T(8,128)(2,1)S(1)}, bf16[1536,512]{1,0:T(8,128)(2,1)S(1)}, bf16[1536,512]{1,0:T(8,128)(2,1)S(1)}) custom-call(s32[96]{0:T(128)} %owner.3, bf16[2,12,4,16,512]{4,3,2,1,0:T(8,128)(2,1)} %bitcast.3, bf16[16,512]{1,0:T(8,128)(2,1)} %left.1, bf16[16,512]{1,0:T(8,128)(2,1)} %right.1), custom_call_target="tpu_custom_call" | custom-call | tf_op jit(solution)/shard_map/pallas_call | solution.py:344
  55.4 0.0 copy-done.2
  55.4 0.0 copy-done.1
  55.4 0.0 copy-done
  55.4 4.1 %shard_map.86 = (bf16[1536,512]{1,0:T(8,128)(2,1)}, f32[16,512]{1,0:T(8,128)}, f32[16,512]{1,0:T(8,128)}) custom-call(s32[96]{0:T(128)S(1)} %copy-done.2, bf16[1536,512]{1,0:T(8,128)(2,1)S(1)} %bitcast.2, bf16[1536,512]{1,0:T(8,128)(2,1)S(1)} %get-tuple-element.7.pls, bf16[1536,512]{1,0:T(8,128)(2,1)S(1)} %get-tuple-element.8.prs, f32[16,512]{1,0:T(8,128)S(1)} %copy-done, ...), custom_call_target="tpu_custom_call" | custom-call | tf_op jit(solution)/shard_map/pallas_call | solution.py:424
Async XLA Ops:
  0.6 54.7 %copy-start.2 = (s32[96]{0:T(128)S(1)}, s32[96]{0:T(128)}, u32[]{:S(2)}) copy-start(s32[96]{0:T(128)} %owner.3) | copy-start | bytes 1156
  0.6 54.7 %copy-start.1 = (f32[16,512]{1,0:T(8,128)S(1)}, f32[16,512]{1,0:T(8,128)}, u32[]{:S(2)}) copy-start(f32[16,512]{1,0:T(8,128)} %right_factor.1) | copy-start | bytes 98308
  0.7 54.7 %copy-start = (f32[16,512]{1,0:T(8,128)S(1)}, f32[16,512]{1,0:T(8,128)}, u32[]{:S(2)}) copy-start(f32[16,512]{1,0:T(8,128)} %left_factor.1) | copy-start | bytes 98308
